TPU v7x, 256 devices: a whole 4x4x8 slice. The times are simulated.
256 devices in a mesh: facet: 16 (over x, y), span: 16 (over z, core).
Axes of the slice: x: 4, y: 4, z: 8, core: 2. Of those that a mesh axis runs over, the one named last changes fastest.
Arguments:
- visibilities: bfloat16 [16, 512, 2, 1024], P('span', 'facet'), may hold values from -6 to 6
- coordinates: bfloat16 [16, 512, 2, 1024], P('span', 'facet'), may hold values from 4 to 124
- phases: float32 [16, 512, 1024], P('span', 'facet'), may hold values from -3.140625 to 3.140625
- sub_index: int32 [16, 512], replicated, may hold values from 0 to 4095, as said below
Outputs:
- dirty: float32 [8192, 8192], P(('facet', 'span'))
Inputs may be any that keep to these rules, and one draw needn't show every extreme that they name: `sub_index`: within one span (one row) all 512 subgrid indices differ. A grid block is the set of subgrids with rows f * 4 to (f + 1) * 4 - 1 and columns j * 4 to (j + 1) * 4 - 1 for f < 16, j < 16; at most 4 indices of one row fall in one grid block, and in every row some grid block holds exactly 4 of them.
All inputs are finite; a program needn't handle non-finite values.
Results may differ from a plain program's by a relative error of at most 0.005.
Values may be sent and summed in bfloat16 or wider, within the bound.
No kernel may reach another device: no remote copies, remote signals or barrier semaphores. Data moves between devices by JAX's collectives and lax.ppermute only.
A program may use at most 64 MiB of HBM per device.

v0:
```python
import jax
import jax.numpy as jnp
from jax import lax
from jax.sharding import PartitionSpec as P

N = 8192
P_SIZE = 128
CAP = 4


spread = 0.75


def kernel_rows(positions, cell_index):
    gap_size = cell_index - positions[..., None]
    return jnp.exp(-(gap_size * gap_size) / (2.0 * spread * spread))


def subgrids_of(vis_items, coord_items):
    cell_index = jnp.arange(P_SIZE, dtype=jnp.float32)
    coord_vals = coord_items.astype(jnp.float32)
    row_kernel = kernel_rows(coord_vals[:, 0, :], cell_index)
    col_kernel = kernel_rows(coord_vals[:, 1, :], cell_index).astype(jnp.bfloat16)
    weighted = (vis_items.astype(jnp.float32)[:, :, :, None] * row_kernel[:, None, :, :]).astype(
        jnp.bfloat16
    )
    result = jnp.einsum("ezkp,ekq->ezpq", weighted, col_kernel, preferred_element_type=jnp.float32)
    return result.astype(jnp.bfloat16)


def group_subgrids(group_inputs):
    return subgrids_of(group_inputs[0], group_inputs[1])


def entries(sub_row, target, band_sub, col_sub, span_count):
    side_count = N // P_SIZE
    sub_rows = sub_row // side_count
    sub_cols = sub_row % side_count
    owning_block = sub_rows // band_sub * span_count + sub_cols // col_sub
    local_slot = sub_rows % band_sub * col_sub + sub_cols % col_sub
    inside = (owning_block == target).astype(jnp.int32)
    rank_of = jnp.cumsum(inside) - 1
    picked = (
        (inside[None, :] == 1) & (rank_of[None, :] == jnp.arange(CAP, dtype=jnp.int32)[:, None])
    ).astype(jnp.int32)
    block_num = jnp.arange(sub_row.shape[0], dtype=jnp.int32)
    block_ids = jnp.sum(picked * block_num[None, :], axis=1)
    slot_ids = jnp.sum(picked * local_slot[None, :], axis=1)
    filled = jnp.sum(picked, axis=1) > 0
    return (block_ids, slot_ids, filled)


def phase_table(row_count, col_count, length):
    row_ids = jnp.arange(row_count, dtype=jnp.int32)[:, None]
    col_ids = jnp.arange(col_count, dtype=jnp.int32)[None, :]
    angles = 2.0 * jnp.pi / length * (row_ids * col_ids % length).astype(jnp.float32)
    return (jnp.cos(angles), jnp.sin(angles))


def inverse_dft(real_part, imag_part):
    length = real_part.shape[-1]
    first_len = 64
    second_len = length // first_len
    leading = real_part.shape[:-1]
    split_real = real_part.reshape(leading + (first_len, second_len))
    split_imag = imag_part.reshape(leading + (first_len, second_len))
    highest = lax.Precision.HIGHEST
    cos_first, sin_first = phase_table(first_len, first_len, first_len)
    step_real = jnp.einsum(
        "av,...vb->...ab", cos_first, split_real, precision=highest
    ) - jnp.einsum("av,...vb->...ab", sin_first, split_imag, precision=highest)
    step_imag = jnp.einsum(
        "av,...vb->...ab", cos_first, split_imag, precision=highest
    ) + jnp.einsum("av,...vb->...ab", sin_first, split_real, precision=highest)
    cos_twist, sin_twist = phase_table(first_len, second_len, length)
    twist_real = step_real * cos_twist - step_imag * sin_twist
    twist_imag = step_real * sin_twist + step_imag * cos_twist
    cos_second, sin_second = phase_table(second_len, second_len, second_len)
    out_real = jnp.einsum(
        "...ab,bc->...ac", twist_real, cos_second, precision=highest
    ) - jnp.einsum("...ab,bc->...ac", twist_imag, sin_second, precision=highest)
    out_imag = jnp.einsum(
        "...ab,bc->...ac", twist_real, sin_second, precision=highest
    ) + jnp.einsum("...ab,bc->...ac", twist_imag, cos_second, precision=highest)
    out_real = jnp.swapaxes(out_real, -1, -2).reshape(leading + (length,))
    out_imag = jnp.swapaxes(out_imag, -1, -2).reshape(leading + (length,))
    return (out_real, out_imag)


def shards(visibilities, coordinates, phases, sub_index):
    facet_count = lax.axis_size("facet")
    span_count = lax.axis_size("span")
    side_count = N // P_SIZE
    band_sub = side_count // facet_count
    col_sub = side_count // span_count
    facet_id = lax.axis_index("facet")
    span_id = lax.axis_index("span")
    vis_count = visibilities.shape[3]
    vis_float = visibilities.astype(jnp.float32)
    cosine = jnp.cos(phases)
    sine = jnp.sin(phases)
    real_part = vis_float[:, :, 0, :]
    imag_part = vis_float[:, :, 1, :]
    rotated = jnp.stack(
        [real_part * cosine - imag_part * sine, real_part * sine + imag_part * cosine], axis=2
    ).astype(jnp.bfloat16)
    own_row = lax.dynamic_index_in_dim(sub_index, span_id, 0, keepdims=False)
    targets = facet_id * span_count + jnp.arange(span_count, dtype=jnp.int32)

    def send_table(target):
        return entries(own_row, target, band_sub, col_sub, span_count)

    send_ids, send_slots, send_filled = jax.vmap(send_table)(targets)
    flat_ids = send_ids.reshape(-1)
    flat_filled = send_filled.reshape(-1)
    entry_count = flat_ids.shape[0]
    blank = jnp.zeros((entry_count, 2, vis_count), jnp.bfloat16)
    pieces = (
        lax.all_gather(rotated, "facet", axis=1, tiled=True),
        lax.all_gather(coordinates, "facet", axis=1, tiled=True),
    )
    rows_here = pieces[0].shape[1]
    inside = flat_filled & (flat_ids >= 0) & (flat_ids < rows_here)
    where_row = jnp.clip(flat_ids, 0, rows_here - 1)
    vis_rows = jnp.take(pieces[0][0], where_row, axis=0)
    coord_rows = jnp.take(pieces[1][0], where_row, axis=0)
    keep_mask = inside[:, None, None]
    chosen_vis = jnp.where(keep_mask, vis_rows, blank)
    chosen_coords = jnp.where(keep_mask, coord_rows, blank)
    grouped_vis = chosen_vis.reshape(span_count, CAP, 2, vis_count)
    grouped_coords = chosen_coords.reshape(span_count, CAP, 2, vis_count)
    made_subs = lax.map(group_subgrids, (grouped_vis, grouped_coords))
    arrived = lax.all_to_all(made_subs, "span", split_axis=0, concat_axis=0, tiled=True)
    my_block = facet_id * span_count + span_id

    def recv_table(source_row):
        return entries(source_row, my_block, band_sub, col_sub, span_count)

    recv_ids, recv_slots, recv_filled = jax.vmap(recv_table)(sub_index)
    slots_here = band_sub * col_sub
    slot_range = jnp.arange(slots_here, dtype=jnp.int32)[:, None]
    onehot = (
        (recv_slots.reshape(-1)[None, :] == slot_range) & recv_filled.reshape(-1)[None, :]
    ).astype(jnp.bfloat16)
    items = arrived.reshape(span_count * CAP, 2 * P_SIZE * P_SIZE)
    summed = jnp.dot(onehot, items, preferred_element_type=jnp.float32)
    block = (
        summed.reshape(band_sub, col_sub, 2, P_SIZE, P_SIZE)
        .transpose(2, 0, 3, 1, 4)
        .reshape(2, band_sub * P_SIZE, col_sub * P_SIZE)
    )
    row_block = lax.all_to_all(block, "span", split_axis=1, concat_axis=2, tiled=True)
    half_real, half_imag = inverse_dft(row_block[0], row_block[1])
    half_done = jnp.stack([half_real, half_imag])
    columns = lax.all_to_all(
        lax.all_to_all(half_done, "facet", split_axis=2, concat_axis=1, tiled=True),
        "span",
        split_axis=2,
        concat_axis=1,
        tiled=True,
    )
    row_count = half_done.shape[1]
    col_count = columns.shape[2]
    ordered = (
        columns.reshape(2, span_count, facet_count, row_count, col_count)
        .transpose(0, 4, 2, 1, 3)
        .reshape(2, col_count, N)
    )
    image_real, image_imag = inverse_dft(ordered[0], ordered[1])
    return image_real * (1.0 / N)


def solution(mesh):
    return jax.shard_map(
        shards,
        mesh=mesh,
        in_specs=(
            P("span", "facet", None, None),
            P("span", "facet", None, None),
            P("span", "facet", None),
            P(),
        ),
        out_specs=P(("facet", "span"), None),
        check_vma=False,
    )
```

profile of v0, /device:TPU:1, one launch (start us, length us, event | category | flops | bytes accessed | tf_op | source)
XLA Modules:
  0.0 588.6 jit_solution(86421095488678001)
XLA Ops:
  12.9 49.8 %all-gather.5.cloned.1.call-done = bf16[1,512,2,1024]{3,2,0,1:T(2,128)(2,1)} async-done(((bf16[1,32,2,1024]{3,2,0,1:T(2,128)(2,1)}), bf16[1,512,2,1024]{3,2,0,1:T(2,128)(2,1)}) %all-gather.5.cloned.1.call-update) | async-done | bytes 2097168 | tf_op jit(solution)/shard_map/all_gather | solution.py:120
  62.7 2.7 gather_fusion.1
  65.4 49.1 %all-gather.3.cloned.1.call-done = bf16[1,512,2,1024]{3,2,0,1:T(2,128)(2,1)} async-done(((bf16[1,32,2,1024]{3,2,0,1:T(2,128)(2,1)}), bf16[1,512,2,1024]{3,2,0,1:T(2,128)(2,1)}) %all-gather.3.cloned.1.call-update) | async-done | bytes 2097168 | tf_op jit(solution)/shard_map/all_gather | solution.py:119
  114.6 2.7 gather_fusion
  117.9 90.2 %while.10 = (s32[]{:T(128)}, bf16[16,4,2,128,128]{4,3,2,1,0:T(8,128)(2,1)}, bf16[16,4,2,1024]{3,2,1,0:T(2,128)(2,1)S(1)}, bf16[16,4,2,1024]{3,2,1,0:T(2,128)(2,1)S(1)}, s32[]{:T(128)}) while((s32[]{:T(128)}, bf16[16,4,2,128,128]{4,3,2,1,0:T(8,128)(2,1)}, bf16[16,4,2,1024]{3,2,1,0:T(2,128)(2,1)S(1)}, bf16[16,4,2,1024]{3,2,1,0:T(2,128)(2,1)S(1)}, ...), condition=%wide.region_9.11_spmd, body=%wide.region_8.10_spmd.sunk | while | flops 275398656 | bytes 8912977 | solution.py:132
  120.5 3.1 fusion.190
  126.2 3.1 fusion.190
  131.8 3.1 fusion.190
  137.4 3.1 fusion.190
  143.1 3.1 fusion.190
  148.7 3.1 fusion.190
  154.3 3.1 fusion.190
  160.0 3.1 fusion.190
  165.6 3.1 fusion.190
  171.2 3.1 fusion.190
  176.9 3.1 fusion.190
  182.5 3.1 fusion.190
  188.1 3.1 fusion.190
  193.8 3.1 fusion.190
  199.4 3.1 fusion.190
  205.0 3.1 fusion.190
  208.1 8.5 %all-to-all-start = ((bf16[16,4,2,128,128]{4,3,2,1,0:T(8,128)(2,1)}), bf16[16,4,2,128,128]{4,3,2,1,0:T(8,128)(2,1)}, u32[]{:S(2)}, u32[]{:S(2)}) async-start(bf16[16,4,2,128,128]{4,3,2,1,0:T(8,128)(2,1)} %get-tuple-element.28), calls=%async_computation | async-start | bytes 8388608 | tf_op jit(solution)/shard_map/all_to_all | solution.py:133
  218.9 91.3 %all-to-all-done = bf16[16,4,2,128,128]{4,3,2,1,0:T(8,128)(2,1)} async-done(((bf16[16,4,2,128,128]{4,3,2,1,0:T(8,128)(2,1)}), bf16[16,4,2,128,128]{4,3,2,1,0:T(8,128)(2,1)}, u32[]{:S(2)}, u32[]{:S(2)}) %all-to-all-start) | async-done | bytes 4194336 | tf_op jit(solution)/shard_map/all_to_all | solution.py:133
  310.2 7.3 %reshape.280 = bf16[64,32768]{1,0:T(8,128)(2,1)} reshape(bf16[16,4,2,128,128]{4,3,2,1,0:T(8,128)(2,1)} %all-to-all-done) | data formatting | bytes 8388608 | tf_op jit(solution)/shard_map/reshape | solution.py:145
  317.5 3.3 copy.148
  320.9 2.6 fusion.15
  323.8 2.6 reshape.314
  326.5 5.8 all-to-all-start.1
  332.4 48.7 %all-to-all-done.1 = f32[2,512,512]{2,0,1:T(2,128)S(1)} async-done(((f32[2,512,512]{2,0,1:T(2,128)}), f32[2,512,512]{2,0,1:T(2,128)S(1)}, u32[]{:S(2)}, u32[]{:S(2)}) %all-to-all-start.1) | async-done | bytes 2097184 | tf_op jit(solution)/shard_map/all_to_all | solution.py:152
  382.5 2.1 fusion.76
  390.1 2.2 fusion.38
  393.6 2.0 copy.129
  395.5 2.3 stack_reshape.7
  397.9 3.4 fusion.23
  406.1 7.9 %copy.130 = f32[2,32,8192]{1,0,2:T(2,128)} copy(f32[2,32,8192]{2,1,0:T(8,128)S(1)} %pad_maximum_fusion) | data formatting | bytes 4194304 | tf_op jit(solution)/shard_map/stack | solution.py:154
  414.0 10.3 %reshape.317 = f32[16,1,32768]{2,1,0:T(1,128)S(1)} reshape(f32[8192,2,32]{2,1,0:T(2,128)} %bitcast.179) | data formatting | bytes 4194304
  424.3 31.8 %all_to_all.53 = f32[16,1,32768]{2,1,0:T(1,128)} all-to-all(f32[16,1,32768]{2,1,0:T(1,128)S(1)} %reshape.317), channel_id=1, replica_groups=mesh['facet'=16,'span'=16] {'facet'}, dimensions={0} | all-to-all | bytes 4194304 | tf_op jit(solution)/shard_map/all_to_all | solution.py:156
  456.6 7.3 %reduce.4 = f32[16,32768]{1,0:T(8,128)S(1)} reduce(f32[16,1,32768]{2,1,0:T(1,128)} %all_to_all.53, f32[]{:T(128)} %broadcast.473), dimensions={1}, to_apply=%all_to_all.42.reduce_sub_computation | reduce | bytes 4194308 | tf_op jit(solution)/shard_map/all_to_all | solution.py:156
  463.9 9.0 %reshape.318 = f32[8192,2,32]{2,1,0:T(2,128)} reshape(f32[16,32768]{1,0:T(8,128)S(1)} %reduce.4) | data formatting | bytes 4194304
  472.9 10.2 %copy.142 = f32[2,32,16,512]{3,1,2,0:T(8,128)S(1)} copy(f32[2,32,16,512]{1,0,3,2:T(2,128)} %bitcast.180) | data formatting | bytes 4194304 | tf_op jit(solution)/shard_map/all_to_all | solution.py:156
  483.1 2.5 copy.133
  485.6 58.1 %all_to_all.54 = f32[2,512,512]{1,0,2:T(2,128)S(1)} all-to-all(f32[2,512,512]{1,0,2:T(2,128)} %copy.133), channel_id=1, replica_groups=mesh['facet'=16,'span'=16] {'span'}, dimensions={2} | all-to-all | bytes 4194304 | tf_op jit(solution)/shard_map/all_to_all | solution.py:155
  544.0 4.4 reshape.282
  548.5 6.1 %fusion.174 = (f32[1,32,16,16,32]{4,2,1,3,0:T(8,128)S(1)}, f32[1,32,16,16,32]{4,2,1,3,0:T(8,128)}) fusion(f32[2,32,16,16,32]{4,2,1,3,0:T(8,128)} %bitcast.181), kind=kLoop, calls=%fused_computation.251 | loop fusion | bytes 4194304 | tf_op jit(solution)/shard_map/slice | solution.py:169
  554.6 4.4 copy.135
  558.9 3.3 reshape_squeeze.14
  563.4 6.5 %copy.136 = f32[1,32,16,16,32]{4,3,2,1,0:T(8,128)} copy(f32[1,32,16,16,32]{4,2,1,3,0:T(8,128)} %get-tuple-element.70) | data formatting | bytes 2097152 | tf_op jit(solution)/shard_map/slice | solution.py:169
  569.9 3.4 reshape_squeeze.15
  (171 shorter events, 73.1 us)
Async XLA Ops:
  6.5 4.0 copy-start.1
  6.5 56.2 %all-gather.5.cloned.1.call-start = ((), (), s32[]{:S(2)}) async-start(), calls=%async_computation.5 | async-start | bytes 2228224 | tf_op jit(solution)/shard_map/all_gather | solution.py:120
  7.3 107.3 %all-gather.3.cloned.1.call-start = ((), (), s32[]{:S(2)}) async-start(), calls=%async_computation.4 | async-start | bytes 2228224 | tf_op jit(solution)/shard_map/all_gather | solution.py:119
  208.1 102.1 %all-to-all-start = ((bf16[16,4,2,128,128]{4,3,2,1,0:T(8,128)(2,1)}), bf16[16,4,2,128,128]{4,3,2,1,0:T(8,128)(2,1)}, u32[]{:S(2)}, u32[]{:S(2)}) async-start(bf16[16,4,2,128,128]{4,3,2,1,0:T(8,128)(2,1)} %get-tuple-element.28), calls=%async_computation | async-start | bytes 8388608 | tf_op jit(solution)/shard_map/all_to_all | solution.py:133
  326.5 54.6 %all-to-all-start.1 = ((f32[2,512,512]{2,0,1:T(2,128)}), f32[2,512,512]{2,0,1:T(2,128)S(1)}, u32[]{:S(2)}, u32[]{:S(2)}) async-start(f32[2,512,512]{2,0,1:T(2,128)} %reshape.314), calls=%async_computation.1 | async-start | bytes 4194304 | tf_op jit(solution)/shard_map/all_to_all | solution.py:152
  385.3 1.2 copy-start
Sparse Core Ops, SparseCore 0:
  9.8 52.8 all-gather.4
  65.2 49.3 all-gather.2
where the time goes:
time: 598 us; the launch traced here: 589 us
  waiting for transfers between devices  240 us (40%)
  local copies, waits for them, and re-layouts  133 us (22%)
  blocking collectives  89.9 us (15%)
  matrix products  72.7 us (12%)
  other arithmetic  24.1 us (4%)
  starting transfers between devices  14.4 us (2%)
  between operations  14 us (2%)
    all_to_all x1, waiting for transfers between devices, shards(): lax.all_to_all(made_subs, 'span', split_axis=0, concat_axis=0, tiled=True)  91.3 us
    all_to_all x1, blocking collectives, shards(): lax.all_to_all(lax.all_to_all(half_done, 'facet', split_axis=2, concat_ax...  58.1 us
    all_gather x1, waiting for transfers between devices, shards(): lax.all_gather(coordinates, 'facet', axis=1, tiled=True)  49.8 us
    dot_general x16, matrix products, subgrids_of(): jnp.einsum('ezkp,ekq->ezpq', weighted, col_kernel, preferred_element_type...  49.2 us
    all_gather x1, waiting for transfers between devices, shards(): lax.all_gather(rotated, 'facet', axis=1, tiled=True)  49.1 us
    all_to_all x1, waiting for transfers between devices, shards(): lax.all_to_all(block, 'span', split_axis=1, concat_axis=2, tiled=True)  48.7 us
    all_to_all x1, blocking collectives, shards(): lax.all_to_all(half_done, 'facet', split_axis=2, concat_axis=1, tiled=True)  31.8 us
    exp x16, local copies, waits for them, and re-layouts, kernel_rows(): return jnp.exp(-(gap_size * gap_size) / (2.0 * spread * spread))  29.8 us
  transfers between devices with their start and end apart: 4, of which 4 were waited for; matrix products, arithmetic and copies ran while one was open for 2% of the time, Pallas kernels for 0%

commit v1 on v0

v1 whole, which is shorter than its diff:
```python
import numpy as np
import jax
import jax.numpy as jnp
from jax import lax
from jax.experimental import pallas as pl
from jax.experimental.pallas import tpu as pltpu
from jax.sharding import PartitionSpec as P

N = 8192
P_SIZE = 128
CAP = 4
SIDE = N // P_SIZE
BAND = 4
SPREAD = 0.75
F32 = jnp.float32
BF16 = jnp.bfloat16
GAUSS = -1.0 / (2.0 * SPREAD * SPREAD * np.log(2.0))
VMEM_LIMIT = 56 * 1024 * 1024


def angle_tables(rows, cols, length):
    angles = 2.0 * np.pi * ((rows[:, None] * cols[None, :]) % length) / length
    return np.cos(angles), np.sin(angles)


def complex_matrix(cosine, sine):
    return np.block([[cosine, -sine], [sine, cosine]])


def split_table(table):
    high = table.astype(np.float32).astype(BF16)
    low = (table - high.astype(np.float64)).astype(np.float32).astype(BF16)
    return high, low


def row_tables():
    dft_hi, dft_lo = split_table(
        complex_matrix(*angle_tables(np.arange(128), np.arange(128), 128))
    )
    twist_cos, twist_sin = angle_tables(np.arange(64), np.arange(128), N)
    return dft_hi, dft_lo, twist_cos.astype(np.float32), twist_sin.astype(np.float32)


def column_tables():
    order = (np.arange(256) % 16) * 16 + np.arange(256) // 16
    first = complex_matrix(*angle_tables(np.arange(256), order, 256)) / N
    first_hi, first_lo = split_table(first)
    lane_r = np.arange(128) % 32
    twist_cos, twist_sin = angle_tables(np.arange(256), lane_r, N)
    cos_r, sin_r = angle_tables(np.arange(32), np.arange(32), 32)
    last = np.concatenate(
        [np.kron(np.eye(4), cos_r), -np.kron(np.eye(4), sin_r)], axis=1
    )
    last_hi, last_lo = split_table(last)
    return (
        first_hi,
        first_lo,
        twist_cos.astype(np.float32),
        twist_sin.astype(np.float32),
        last_hi,
        last_lo,
    )


def split_value(value):
    high = value.astype(BF16)
    low = (value - high.astype(F32)).astype(BF16)
    return high, low


def nt_dot(left, right):
    return lax.dot_general(
        left, right, (((1,), (1,)), ((), ())), preferred_element_type=F32
    )


def pick_kernel(ids_ref, source_ref, out_ref, sem):
    count = out_ref.shape[0]

    def start(i, carry):
        pltpu.make_async_copy(source_ref.at[ids_ref[i]], out_ref.at[i], sem).start()
        return carry

    lax.fori_loop(0, count, start, 0)
    pltpu.make_async_copy(source_ref.at[pl.ds(0, count)], out_ref, sem).wait()


def pick_blocks(ids, source):
    count = ids.shape[0]
    return pl.pallas_call(
        pick_kernel,
        out_shape=jax.ShapeDtypeStruct((count,) + source.shape[1:], source.dtype),
        grid_spec=pltpu.PrefetchScalarGridSpec(
            num_scalar_prefetch=1,
            grid=(1,),
            in_specs=[pl.BlockSpec(memory_space=pl.ANY)],
            out_specs=pl.BlockSpec(memory_space=pl.ANY),
            scratch_shapes=[pltpu.SemaphoreType.DMA],
        ),
        name="pick_blocks",
    )(ids, source)


def grid_kernel(order_ref, slot_ref, count_ref, vis_ref, out_ref, acc_ref):
    acc_ref[...] = jnp.zeros_like(acc_ref)
    cells = lax.broadcasted_iota(jnp.int32, (P_SIZE, 128), 0).astype(F32)
    count = count_ref[0]

    def one_block(at, live):
        entry = order_ref[at]
        slot = slot_ref[at]
        values = vis_ref[entry].astype(F32)
        keep = jnp.where(live, 1.0, 0.0).astype(F32)
        real = values[0:8] * keep
        imag = values[8:16] * keep
        place_u = values[16:24]
        place_v = values[24:32]
        total = jnp.zeros((2 * P_SIZE, P_SIZE), F32)
        for pair in range(4):
            left = []
            right = []
            for k in (2 * pair, 2 * pair + 1):
                gap_u = cells - place_u[k : k + 1]
                row = jnp.exp2(gap_u * gap_u * GAUSS)
                left.append(
                    jnp.concatenate(
                        [
                            (real[k : k + 1] * row).astype(BF16),
                            (imag[k : k + 1] * row).astype(BF16),
                        ],
                        axis=0,
                    )
                )
                gap_v = cells - place_v[k : k + 1]
                right.append(jnp.exp2(gap_v * gap_v * GAUSS).astype(BF16))
            total += nt_dot(
                jnp.concatenate(left, axis=1), jnp.concatenate(right, axis=1)
            )
        acc_ref[slot] += total.astype(BF16).astype(F32)

    def step(i, carry):
        one_block(2 * i, True)
        one_block(2 * i + 1, 2 * i + 1 < count)
        return carry

    lax.fori_loop(0, (count + 1) // 2, step, 0)
    for slot in range(BAND * BAND):
        sub_row, sub_col = divmod(slot, BAND)
        for part in range(2):
            for piece in range(4):
                start = part * P_SIZE + piece * 32
                out_ref[
                    4 * sub_row + piece, part, :, sub_col * P_SIZE : (sub_col + 1) * P_SIZE
                ] = acc_ref[slot, start : start + 32, :].astype(BF16)


def grid_blocks(order, slots, count, vis):
    whole = lambda *_: (0, 0, 0)
    return pl.pallas_call(
        grid_kernel,
        out_shape=jax.ShapeDtypeStruct((16, 2, 32, 512), BF16),
        grid_spec=pltpu.PrefetchScalarGridSpec(
            num_scalar_prefetch=3,
            grid=(1,),
            in_specs=[pl.BlockSpec(vis.shape, whole)],
            out_specs=pl.BlockSpec((16, 2, 32, 512), lambda *_: (0, 0, 0, 0)),
            scratch_shapes=[pltpu.VMEM((BAND * BAND, 2 * P_SIZE, P_SIZE), F32)],
        ),
        compiler_params=pltpu.CompilerParams(vmem_limit_bytes=VMEM_LIMIT),
        name="grid_blocks",
    )(order, slots, count, vis)


def add(x, y):
    return x[0] + y[0], x[1] + y[1]


def sub(x, y):
    return x[0] - y[0], x[1] - y[1]


def turn(x):
    return -x[1], x[0]


def scale(x, numer, denom):
    numer %= denom
    if numer == 0:
        return x
    if 4 * numer == denom:
        return turn(x)
    if 2 * numer == denom:
        return -x[0], -x[1]
    if 4 * numer == 3 * denom:
        return x[1], -x[0]
    cosine = float(np.cos(2 * np.pi * numer / denom))
    sine = float(np.sin(2 * np.pi * numer / denom))
    return x[0] * cosine - x[1] * sine, x[0] * sine + x[1] * cosine


def dft4(x0, x1, x2, x3):
    even_sum, even_diff = add(x0, x2), sub(x0, x2)
    odd_sum, odd_diff = add(x1, x3), turn(sub(x1, x3))
    return (
        add(even_sum, odd_sum),
        add(even_diff, odd_diff),
        sub(even_sum, odd_sum),
        sub(even_diff, odd_diff),
    )


def dft16(items):
    firsts = [dft4(*[items[4 * j1 + j2] for j1 in range(4)]) for j2 in range(4)]
    result = [None] * 16
    for b1 in range(4):
        lasts = dft4(*[scale(firsts[j2][b1], j2 * b1, 16) for j2 in range(4)])
        for b2 in range(4):
            result[b1 + 4 * b2] = lasts[b2]
    return result


def row_kernel(
    x_ref, dft_hi_ref, dft_lo_ref, cos_ref, sin_ref, out_ref, mid_ref, hi_ref, lo_ref, put_ref
):
    for half in range(2):
        rows = pl.ds(16 * half, 16)
        for kappa in range(4):
            lanes = pl.ds(128 * kappa, 128)
            items = [
                (x_ref[j, 0, rows, lanes].astype(F32), x_ref[j, 1, rows, lanes].astype(F32))
                for j in range(16)
            ]
            for a1, item in enumerate(dft16(items)):
                item = scale(item, kappa * a1, 64)
                mid_ref[kappa, a1, 0, rows, :] = item[0]
                mid_ref[kappa, a1, 1, rows, :] = item[1]
    for a1 in range(16):
        items = [(mid_ref[kappa, a1, 0], mid_ref[kappa, a1, 1]) for kappa in range(4)]
        for a2, item in enumerate(dft4(*items)):
            a = a1 + 16 * a2
            cosine = cos_ref[a : a + 1, :]
            sine = sin_ref[a : a + 1, :]
            real = item[0] * cosine - item[1] * sine
            imag = item[0] * sine + item[1] * cosine
            both = jnp.concatenate([real, imag], axis=1)
            high, low = split_value(both)
            hi_ref[a * 32 : (a + 1) * 32, :] = high
            lo_ref[a * 32 : (a + 1) * 32, :] = low
    dft_hi = dft_hi_ref[...]
    dft_lo = dft_lo_ref[...]
    for n in range(8):
        high = hi_ref[n * 256 : (n + 1) * 256, :]
        low = lo_ref[n * 256 : (n + 1) * 256, :]
        made = nt_dot(dft_hi, high) + nt_dot(dft_lo, high) + nt_dot(dft_hi, low)
        for part in range(2):
            for piece in range(2):
                half, i = divmod(2 * n + piece, 8)
                put_ref[pl.ds(half * 16 + part * 8 + i, 128, stride=32), :] = made[
                    part * 128 : (part + 1) * 128, piece * 128 : (piece + 1) * 128
                ]
    out_ref[...] = put_ref[...].reshape(256, 16, 128).astype(BF16)


def row_transform(x):
    tables = [jnp.asarray(t) for t in row_tables()]
    return pl.pallas_call(
        row_kernel,
        out_shape=jax.ShapeDtypeStruct((256, 16, 128), BF16),
        scratch_shapes=[
            pltpu.VMEM((4, 16, 2, 32, 128), F32),
            pltpu.VMEM((2048, 256), BF16),
            pltpu.VMEM((2048, 256), BF16),
            pltpu.VMEM((4096, 128), F32),
        ],
        compiler_params=pltpu.CompilerParams(vmem_limit_bytes=VMEM_LIMIT),
        name="row_transform",
    )(x, *tables)


def column_kernel(
    x_ref, first_hi_ref, first_lo_ref, cos_ref, sin_ref, last_hi_ref, last_lo_ref, out_ref, get_ref, put_ref
):
    get_ref[...] = x_ref[...].astype(F32).reshape(4096, 128)
    first_hi = first_hi_ref[...]
    first_lo = first_lo_ref[...]
    last_hi = last_hi_ref[...]
    last_lo = last_lo_ref[...]
    cosine = cos_ref[...]
    sine = sin_ref[...]
    for g in range(8):
        x = jnp.concatenate(
            [
                get_ref[pl.ds(g, 256, stride=16), :].astype(BF16),
                get_ref[pl.ds(8 + g, 256, stride=16), :].astype(BF16),
            ],
            axis=0,
        )
        mid = jnp.dot(first_hi, x, preferred_element_type=F32) + jnp.dot(
            first_lo, x, preferred_element_type=F32
        )
        real, imag = mid[:256], mid[256:]
        both = jnp.concatenate(
            [real * cosine - imag * sine, real * sine + imag * cosine], axis=1
        )
        high, low = split_value(both)
        made = nt_dot(last_hi, high) + nt_dot(last_lo, high) + nt_dot(last_hi, low)
        for side in range(2):
            start = side * 1024 + g * 128
            put_ref[start : start + 128, :] = made[:, side * 128 : (side + 1) * 128]
    for gamma in range(32):
        for side in range(2):
            start = gamma * 256 + side * 128
            out_ref[:, start : start + 128] = put_ref[
                pl.ds(side * 1024 + gamma, 32, stride=32), :
            ]


def column_transform(x):
    tables = [jnp.asarray(t) for t in column_tables()]
    return pl.pallas_call(
        column_kernel,
        out_shape=jax.ShapeDtypeStruct((32, N), F32),
        scratch_shapes=[pltpu.VMEM((4096, 128), F32), pltpu.VMEM((2048, 128), F32)],
        compiler_params=pltpu.CompilerParams(vmem_limit_bytes=VMEM_LIMIT),
        name="column_transform",
    )(x, *tables)


def block_of(index):
    row = index // SIDE
    col = index % SIDE
    return row // BAND, col // BAND, row % BAND * BAND + col % BAND


def send_ids(own_row, facet_id):
    band, column, slot = block_of(own_row)
    key = band * 16 + column
    number = jnp.arange(own_row.shape[0], dtype=jnp.int32)
    same = (key[None, :] == key[:, None]) & (number[None, :] < number[:, None])
    rank = jnp.sum(same.astype(jnp.int32), axis=1)
    want_band = jnp.repeat(jnp.arange(16, dtype=jnp.int32), CAP)[:, None]
    want_rank = jnp.tile(jnp.arange(CAP, dtype=jnp.int32), 16)[:, None]
    hit = (key[None, :] == want_band * 16 + facet_id) & (rank[None, :] == want_rank)
    return jnp.sum(jnp.where(hit, number[None, :], 0), axis=1)


def receive_table(sub_index, my_band, my_column):
    band, column, slot = block_of(sub_index)
    inside = (band == my_band) & (column == my_column)
    count = sub_index.shape[1]
    before = (
        jnp.arange(count)[:, None] < jnp.arange(count)[None, :]
    ).astype(BF16)
    rank = jnp.dot(inside.astype(BF16), before, preferred_element_type=F32)
    hit = inside[:, None, :] & (rank[:, None, :] == jnp.arange(CAP, dtype=F32)[None, :, None])
    filled = jnp.any(hit, axis=2).reshape(-1)
    slots = jnp.sum(jnp.where(hit, slot[:, None, :], 0), axis=2).reshape(-1)
    entries = filled.shape[0]
    number = jnp.arange(entries, dtype=jnp.int32)
    place = jnp.sum(
        ((number[None, :] < number[:, None]) & filled[None, :]).astype(jnp.int32), axis=1
    )
    chosen = filled[None, :] & (place[None, :] == number[:, None])
    order = jnp.sum(jnp.where(chosen, number[None, :], 0), axis=1)
    sorted_slots = jnp.sum(jnp.where(chosen, slots[None, :], 0), axis=1)
    total = jnp.sum(filled.astype(jnp.int32)).reshape(1)
    return order, sorted_slots, total


def shards(visibilities, coordinates, phases, sub_index):
    facet_id = lax.axis_index("facet")
    span_id = lax.axis_index("span")
    blocks = visibilities.shape[1]
    with jax.named_scope("rotate"):
        vis = visibilities[0].reshape(blocks, 2, 8, 128).astype(F32)
        place = coordinates[0].reshape(blocks, 16, 128)
        angle = phases[0].reshape(blocks, 8, 128)
        cosine = jnp.cos(angle)
        sine = jnp.sin(angle)
        real = vis[:, 0] * cosine - vis[:, 1] * sine
        imag = vis[:, 0] * sine + vis[:, 1] * cosine
        records = jnp.concatenate([real.astype(BF16), imag.astype(BF16), place], axis=1)
    with jax.named_scope("gather_span"):
        everything = lax.all_gather(records, "facet", axis=0, tiled=True)
    with jax.named_scope("choose"):
        own_row = lax.dynamic_index_in_dim(sub_index, span_id, 0, keepdims=False)
        chosen = pick_blocks(send_ids(own_row, facet_id), everything)
        order, slots, count = receive_table(sub_index, span_id, facet_id)
    with jax.named_scope("to_owner"):
        arrived = lax.all_to_all(
            chosen.reshape(16, CAP, 32, 128), "span", split_axis=0, concat_axis=0, tiled=True
        )
    with jax.named_scope("gridding"):
        block = grid_blocks(order, slots, count, arrived.reshape(16 * CAP, 32, 128))
    with jax.named_scope("to_rows"):
        rows = lax.all_to_all(block, "facet", split_axis=0, concat_axis=0, tiled=True)
    with jax.named_scope("rows_dft"):
        half_done = row_transform(rows)
    with jax.named_scope("to_columns"):
        columns = lax.all_to_all(
            half_done, ("facet", "span"), split_axis=0, concat_axis=0, tiled=True
        )
    with jax.named_scope("columns_dft"):
        return column_transform(columns)


def solution(mesh):
    return jax.shard_map(
        shards,
        mesh=mesh,
        in_specs=(
            P("span", "facet", None, None),
            P("span", "facet", None, None),
            P("span", "facet", None),
            P(),
        ),
        out_specs=P(("facet", "span"), None),
        check_vma=False,
    )
```

time: 598 us -> 217 us (0.36); the launches traced: 589 us -> 216 us
  waiting for transfers between devices: 240 us -> 72.5 us
  local copies, waits for them, and re-layouts: 133 us -> 4.73 us
  matrix products: 72.7 us -> 0.18 us
  Pallas kernels: 0 us -> 43.8 us
  blocking collectives: 89.9 us -> 68.3 us
  other arithmetic: 24.1 us -> 5.3 us
  starting transfers between devices: 14.4 us -> 7.71 us
    all_to_all x2 -> x1, waiting for transfers between devices: 140 us -> 14.8 us  [shards(): lax.all_to_all(chosen.reshape(16, CAP, 32, 128), 'span', split_axis=0, co...]
    dot_general x31 -> x1, matrix products: 72.7 us -> 0.18 us  [receive_table(): rank = jnp.dot(inside.astype(BF16), before, preferred_element_type=F32)]
    pallas_call x0 -> x4, Pallas kernels: none -> 43.8 us  [the longest x1 17.7 us: pick_blocks(): pl.pallas_call(pick_kernel, out_shape=jax.ShapeDtypeStruct((count,) + sou...]
    all_gather x2 -> x1, waiting for transfers between devices: 99 us -> 57.7 us  [shards(): everything = lax.all_gather(records, 'facet', axis=0, tiled=True)]
    exp x16 -> x0, local copies, waits for them, and re-layouts: 29.8 us -> none  [kernel_rows(): return jnp.exp(-(gap_size * gap_size) / (2.0 * spread * spread))]
    all_to_all x2, blocking collectives: 89.9 us -> 68.3 us  [the longest x1 49.5 us: shards(): lax.all_to_all(half_done, ('facet', 'span'), split_axis=0, concat_axis=0,...]
    unnamed x7, local copies, waits for them, and re-layouts: 22.7 us -> 2.22 us
    another operation x11 -> x1, local copies, waits for them, and re-layouts: 19.7 us -> 0.01 us  [send_ids(): want_rank = jnp.tile(jnp.arange(CAP, dtype=jnp.int32), 16)[:, None]]
  transfers between devices with their start and end apart: 4 -> 2, of which waited for: 4 -> 2; matrix products, arithmetic and copies ran while one was open for 2% -> 2% of each run, Pallas kernels for 0% -> 0%
where the time goes in v1:
time: 217 us; the launch traced here: 216 us
  waiting for transfers between devices  72.5 us (33%)
  blocking collectives  68.3 us (31%)
  Pallas kernels  43.8 us (20%)
  between operations  13.5 us (6%)
  starting transfers between devices  7.71 us (4%)
  other arithmetic  5.3 us (2%)
  local copies, waits for them, and re-layouts  4.73 us (2%)
    all_gather x1, waiting for transfers between devices, shards(): everything = lax.all_gather(records, 'facet', axis=0, tiled=True)  57.7 us
    all_to_all x1, blocking collectives, shards(): lax.all_to_all(half_done, ('facet', 'span'), split_axis=0, concat_axis=0,...  49.5 us
    all_to_all x1, blocking collectives, shards(): lax.all_to_all(block, 'facet', split_axis=0, concat_axis=0, tiled=True)  18.8 us
    pallas_call x1, Pallas kernels, pick_blocks(): pl.pallas_call(pick_kernel, out_shape=jax.ShapeDtypeStruct((count,) + sou...  17.7 us
    all_to_all x1, waiting for transfers between devices, shards(): lax.all_to_all(chosen.reshape(16, CAP, 32, 128), 'span', split_axis=0, co...  14.8 us
    pallas_call x1, Pallas kernels, grid_blocks(): pl.pallas_call(grid_kernel, out_shape=jax.ShapeDtypeStruct((16, 2, 32, 51...  10.5 us
    pallas_call x1, Pallas kernels, column_transform(): pl.pallas_call(column_kernel, out_shape=jax.ShapeDtypeStruct((32, N), F32...  10.3 us
    all_to_all x1, starting transfers between devices, shards(): lax.all_to_all(chosen.reshape(16, CAP, 32, 128), 'span', split_axis=0, co...  7.71 us
  transfers between devices with their start and end apart: 2, of which 2 were waited for; matrix products, arithmetic and copies ran while one was open for 2% of the time, Pallas kernels for 0%

profile of v1, /device:TPU:1, one launch (start us, length us, event | category | flops | bytes accessed | tf_op | source)
XLA Modules:
  0.0 216.1 jit_solution(10414430756157533480)
XLA Ops:
  6.5 0.0 all-gather.2.cloned.1.call-start
  6.5 1.0 squeeze.20
  7.5 1.0 reshape.123
  8.5 1.4 cosine_bitcast_fusion
  9.9 0.0 copy-start.1
  10.0 0.7 pad_maximum_fusion
  10.8 0.0 all-gather.2.cloned.1.call-update
  10.8 0.1 add.91
  10.9 0.1 eq.102
  11.0 0.8 fusion.25
  11.8 0.2 convert_reduce_fusion
  12.0 0.7 select_reduce_fusion.ids_ref
  12.7 0.8 fusion.17
  13.6 57.7 %all-gather.2.cloned.1.call-done.source_ref = bf16[512,32,128]{2,1,0:T(8,128)(2,1)} async-done(((bf16[32,32,128]{2,1,0:T(8,128)(2,1)}), bf16[512,32,128]{2,1,0:T(8,128)(2,1)}) %all-gather.2.cloned.1.call-update) | async-done | bytes 4194320 | tf_op jit(solution)/shard_map/gather_span/all_gather | solution.py:384
  71.3 17.7 %pick_blocks.1 = bf16[64,32,128]{2,1,0:T(8,128)(2,1)} custom-call(s32[64]{0:T(128)} %select_reduce_fusion.ids_ref, bf16[512,32,128]{2,1,0:T(8,128)(2,1)} %all-gather.2.cloned.1.call-done.source_ref), custom_call_target="tpu_custom_call" | custom-call | tf_op jit(solution)/shard_map/choose/pick_blocks/pallas_call | solution.py:90
  89.0 7.7 %all-to-all-start = ((bf16[16,4,32,128]{3,2,1,0:T(8,128)(2,1)}), bf16[16,4,32,128]{3,2,1,0:T(8,128)(2,1)S(1)}, u32[]{:S(2)}, u32[]{:S(2)}) async-start(bf16[16,4,32,128]{3,2,1,0:T(8,128)(2,1)} %bitcast.47), calls=%async_computation | async-start | bytes 1048576 | tf_op jit(solution)/shard_map/to_owner/all_to_all | solution.py:390
  96.7 0.2 fusion.1
  96.8 0.2 fusion.7
  97.0 0.1 copy.18
  97.1 0.1 and.133
  97.2 0.0 copy-done.1
  97.2 0.1 fusion.11
  97.3 0.2 select_reduce_fusion.1
  97.5 0.1 copy.19
  97.5 0.1 broadcast_in_dim.66
  97.6 0.7 convert_reduce_fusion.2
  98.3 0.1 convert_reduce_fusion.1
  98.4 0.7 select_reduce_fusion.2
  99.2 14.8 %all-to-all-done = bf16[16,4,32,128]{3,2,1,0:T(8,128)(2,1)S(1)} async-done(((bf16[16,4,32,128]{3,2,1,0:T(8,128)(2,1)}), bf16[16,4,32,128]{3,2,1,0:T(8,128)(2,1)S(1)}, u32[]{:S(2)}, u32[]{:S(2)}) %all-to-all-start) | async-done | bytes 524320 | tf_op jit(solution)/shard_map/to_owner/all_to_all | solution.py:390
  114.0 0.0 copy-start
  114.0 0.8 copy-done
  114.8 10.5 %grid_blocks.1 = bf16[16,2,32,512]{3,2,1,0:T(8,128)(2,1)} custom-call(s32[64]{0:T(128)} %get-tuple-element.6.order_ref, s32[64]{0:T(128)} %get-tuple-element.5.slot_ref, s32[1]{0:T(128)} %bitcast.count_ref, bf16[64,32,128]{2,1,0:T(8,128)(2,1)} %bitcast.46), custom_call_target="tpu_custom_call" | custom-call | tf_op jit(solution)/shard_map/gridding/grid_blocks/pallas_call | solution.py:159
  125.3 18.8 %all_to_all.15.x_ref = bf16[16,2,32,512]{3,2,1,0:T(8,128)(2,1)} all-to-all(bf16[16,2,32,512]{3,2,1,0:T(8,128)(2,1)} %grid_blocks.1), channel_id=1, replica_groups=mesh['facet'=16,'span'=16] {'facet'}, dimensions={0} | all-to-all | bytes 2097152 | tf_op jit(solution)/shard_map/to_rows/all_to_all | solution.py:396
  144.1 5.3 %row_transform.1 = bf16[256,16,128]{2,1,0:T(8,128)(2,1)} custom-call(bf16[16,2,32,512]{3,2,1,0:T(8,128)(2,1)} %all_to_all.15.x_ref, bf16[256,256]{1,0:T(8,128)(2,1)} %constant.131.clone.dft_hi_ref, bf16[256,256]{1,0:T(8,128)(2,1)} %constant.132.clone.dft_lo_ref, f32[64,128]{1,0:T(8,128)} %constant.133.clone.cos_ref, f32[64,128]{1,0:T(8,128)} %constant.134.clone.sin_ref), custom_call_target="tpu_custom_call" | custom-call | tf_op jit(solution)/shard_map/rows_dft/row_transform/pallas_call | solution.py:266
  149.4 49.5 %all_to_all.16.x_ref = bf16[256,16,128]{2,1,0:T(8,128)(2,1)} all-to-all(bf16[256,16,128]{2,1,0:T(8,128)(2,1)} %row_transform.1), channel_id=1, replica_groups=mesh['facet'=16,'span'=16] {'facet','span'}, dimensions={0} | all-to-all | bytes 2097152 | tf_op jit(solution)/shard_map/to_columns/all_to_all | solution.py:400
  198.9 10.3 %column_transform.1 = f32[32,8192]{1,0:T(8,128)} custom-call(bf16[256,16,128]{2,1,0:T(8,128)(2,1)} %all_to_all.16.x_ref, bf16[512,512]{1,0:T(8,128)(2,1)} %constant.135.clone.first_hi_ref, bf16[512,512]{1,0:T(8,128)(2,1)} %constant.136.clone.first_lo_ref, f32[256,128]{1,0:T(8,128)} %constant.137.clone.cos_ref, f32[256,128]{1,0:T(8,128)} %constant.138.clone.sin_ref, ...), custom_call_target="tpu_custom_call" | custom-call | tf_op jit(solution)/shard_map/columns_dft/column_transform/pallas_call | solution.py:320
  (6 shorter events, 0.1 us)
Async XLA Ops:
  6.5 64.7 %all-gather.2.cloned.1.call-start = ((), (), s32[]{:S(2)}) async-start(), calls=%async_computation.3 | async-start | bytes 4456448 | tf_op jit(solution)/shard_map/gather_span/all_gather | solution.py:384
  9.9 87.3 %copy-start.1 = (s32[16,512]{1,0:T(8,128)S(1)}, s32[16,512]{1,0:T(8,128)}, u32[]{:S(2)}) copy-start(s32[16,512]{1,0:T(8,128)} %param.17) | copy-start | bytes 98308
  89.0 25.0 %all-to-all-start = ((bf16[16,4,32,128]{3,2,1,0:T(8,128)(2,1)}), bf16[16,4,32,128]{3,2,1,0:T(8,128)(2,1)S(1)}, u32[]{:S(2)}, u32[]{:S(2)}) async-start(bf16[16,4,32,128]{3,2,1,0:T(8,128)(2,1)} %bitcast.47), calls=%async_computation | async-start | bytes 1048576 | tf_op jit(solution)/shard_map/to_owner/all_to_all | solution.py:390
  114.0 0.8 copy-start
Sparse Core Ops, SparseCore 0:
  10.9 60.3 all-gather.1

commit v2 on v1

--- a/solution.py
+++ b/solution.py
@@ -9,6 +9,8 @@
 N = 8192
 P_SIZE = 128
 CAP = 4
+STEP = 8
+GAP = 264
 SIDE = N // P_SIZE
 BAND = 4
 SPREAD = 0.75
@@ -42,9 +44,6 @@
 
 
 def column_tables():
-    order = (np.arange(256) % 16) * 16 + np.arange(256) // 16
-    first = complex_matrix(*angle_tables(np.arange(256), order, 256)) / N
-    first_hi, first_lo = split_table(first)
     lane_r = np.arange(128) % 32
     twist_cos, twist_sin = angle_tables(np.arange(256), lane_r, N)
     cos_r, sin_r = angle_tables(np.arange(32), np.arange(32), 32)
@@ -53,10 +52,8 @@
     )
     last_hi, last_lo = split_table(last)
     return (
-        first_hi,
-        first_lo,
-        twist_cos.astype(np.float32),
-        twist_sin.astype(np.float32),
+        (twist_cos / N).astype(np.float32),
+        (twist_sin / N).astype(np.float32),
         last_hi,
         last_lo,
     )
@@ -74,76 +71,93 @@
     )
 
 
-def pick_kernel(ids_ref, source_ref, out_ref, sem):
-    count = out_ref.shape[0]
-
-    def start(i, carry):
-        pltpu.make_async_copy(source_ref.at[ids_ref[i]], out_ref.at[i], sem).start()
-        return carry
-
-    lax.fori_loop(0, count, start, 0)
-    pltpu.make_async_copy(source_ref.at[pl.ds(0, count)], out_ref, sem).wait()
-
-
-def pick_blocks(ids, source):
-    count = ids.shape[0]
+def rotate_kernel(vis0_ref, vis1_ref, u_ref, v_ref, phase_ref, out_ref):
+    for k in range(8):
+        lanes = pl.ds(128 * k, 128)
+        phase = phase_ref[:, lanes]
+        cosine = jnp.cos(phase)
+        sine = jnp.sin(phase)
+        real = vis0_ref[:, lanes].astype(F32)
+        imag = vis1_ref[:, lanes].astype(F32)
+        out_ref[2 * k, :, :128] = (real * cosine - imag * sine).astype(BF16)
+        out_ref[2 * k, :, 128:] = (real * sine + imag * cosine).astype(BF16)
+        out_ref[2 * k + 1, :, :128] = u_ref[:, lanes]
+        out_ref[2 * k + 1, :, 128:] = v_ref[:, lanes]
+
+
+def rotate_blocks(visibilities, coordinates, phases):
+    blocks = phases.shape[0]
+    return pl.pallas_call(
+        rotate_kernel,
+        out_shape=jax.ShapeDtypeStruct((16, blocks, 256), BF16),
+        name="rotate_blocks",
+    )(
+        visibilities[:, 0],
+        visibilities[:, 1],
+        coordinates[:, 0],
+        coordinates[:, 1],
+        phases,
+    )
+
+
+def pick_kernel(code_ref, rows_ref, out_ref, put_ref):
+    wanted = lax.broadcasted_iota(jnp.int32, (256, 512), 0)
+    for piece in range(4):
+        hit = jnp.where(code_ref[...] == wanted + 256 * piece, 1.0, 0.0).astype(BF16)
+        for half in range(2):
+            made = jnp.dot(
+                hit, rows_ref[:, half * 128 : (half + 1) * 128], preferred_element_type=F32
+            )
+            put_ref[pl.ds(512 * piece + half, 256, stride=2), :] = made
+    out_ref[...] = put_ref[...].reshape(256, 8, 128).astype(BF16)
+
+
+def pick_blocks(code, rows):
     return pl.pallas_call(
         pick_kernel,
-        out_shape=jax.ShapeDtypeStruct((count,) + source.shape[1:], source.dtype),
-        grid_spec=pltpu.PrefetchScalarGridSpec(
-            num_scalar_prefetch=1,
-            grid=(1,),
-            in_specs=[pl.BlockSpec(memory_space=pl.ANY)],
-            out_specs=pl.BlockSpec(memory_space=pl.ANY),
-            scratch_shapes=[pltpu.SemaphoreType.DMA],
-        ),
+        out_shape=jax.ShapeDtypeStruct((256, 8, 128), BF16),
+        scratch_shapes=[pltpu.VMEM((2048, 128), F32)],
+        compiler_params=pltpu.CompilerParams(vmem_limit_bytes=VMEM_LIMIT),
         name="pick_blocks",
-    )(ids, source)
-
-
-def grid_kernel(order_ref, slot_ref, count_ref, vis_ref, out_ref, acc_ref):
+    )(code, rows)
+
+
+def grid_kernel(order_ref, slot_ref, count_ref, vis_ref, out_ref, wide_ref, acc_ref):
     acc_ref[...] = jnp.zeros_like(acc_ref)
+    wide_ref[...] = vis_ref[...].astype(F32).reshape(2048, 128)
     cells = lax.broadcasted_iota(jnp.int32, (P_SIZE, 128), 0).astype(F32)
     count = count_ref[0]
 
     def one_block(at, live):
         entry = order_ref[at]
         slot = slot_ref[at]
-        values = vis_ref[entry].astype(F32)
         keep = jnp.where(live, 1.0, 0.0).astype(F32)
-        real = values[0:8] * keep
-        imag = values[8:16] * keep
-        place_u = values[16:24]
-        place_v = values[24:32]
-        total = jnp.zeros((2 * P_SIZE, P_SIZE), F32)
+        first = wide_ref[pl.ds(2 * entry, 16, stride=128), :]
+        second = wide_ref[pl.ds(2 * entry + 1, 16, stride=128), :]
+        total = None
         for pair in range(4):
             left = []
             right = []
             for k in (2 * pair, 2 * pair + 1):
-                gap_u = cells - place_u[k : k + 1]
-                row = jnp.exp2(gap_u * gap_u * GAUSS)
-                left.append(
-                    jnp.concatenate(
-                        [
-                            (real[k : k + 1] * row).astype(BF16),
-                            (imag[k : k + 1] * row).astype(BF16),
-                        ],
-                        axis=0,
-                    )
-                )
-                gap_v = cells - place_v[k : k + 1]
+                real = (first[2 * k : 2 * k + 1] * keep).astype(BF16)
+                imag = (second[2 * k : 2 * k + 1] * keep).astype(BF16)
+                gap_u = cells - first[2 * k + 1 : 2 * k + 2]
+                row = jnp.exp2(gap_u * gap_u * GAUSS).astype(BF16)
+                left.append(jnp.concatenate([row * real, row * imag], axis=0))
+                gap_v = cells - second[2 * k + 1 : 2 * k + 2]
                 right.append(jnp.exp2(gap_v * gap_v * GAUSS).astype(BF16))
-            total += nt_dot(
+            made = nt_dot(
                 jnp.concatenate(left, axis=1), jnp.concatenate(right, axis=1)
             )
+            total = made if total is None else total + made
         acc_ref[slot] += total.astype(BF16).astype(F32)
 
     def step(i, carry):
-        one_block(2 * i, True)
-        one_block(2 * i + 1, 2 * i + 1 < count)
+        for t in range(STEP):
+            one_block(STEP * i + t, STEP * i + t < count)
         return carry
 
-    lax.fori_loop(0, (count + 1) // 2, step, 0)
+    lax.fori_loop(0, (count + STEP - 1) // STEP, step, 0)
     for slot in range(BAND * BAND):
         sub_row, sub_col = divmod(slot, BAND)
         for part in range(2):
@@ -164,7 +178,10 @@
             grid=(1,),
             in_specs=[pl.BlockSpec(vis.shape, whole)],
             out_specs=pl.BlockSpec((16, 2, 32, 512), lambda *_: (0, 0, 0, 0)),
-            scratch_shapes=[pltpu.VMEM((BAND * BAND, 2 * P_SIZE, P_SIZE), F32)],
+            scratch_shapes=[
+                pltpu.VMEM((2048, 128), F32),
+                pltpu.VMEM((BAND * BAND, 2 * P_SIZE, P_SIZE), F32),
+            ],
         ),
         compiler_params=pltpu.CompilerParams(vmem_limit_bytes=VMEM_LIMIT),
         name="grid_blocks",
@@ -278,29 +295,31 @@
 
 
 def column_kernel(
-    x_ref, first_hi_ref, first_lo_ref, cos_ref, sin_ref, last_hi_ref, last_lo_ref, out_ref, get_ref, put_ref
+    x_ref, cos_ref, sin_ref, last_hi_ref, last_lo_ref, out_ref, mid_ref, real_ref, imag_ref, put_ref
 ):
-    get_ref[...] = x_ref[...].astype(F32).reshape(4096, 128)
-    first_hi = first_hi_ref[...]
-    first_lo = first_lo_ref[...]
+    for chunk in range(16):
+        items = []
+        for band in range(16):
+            value = x_ref[chunk * 16 + band].astype(F32)
+            items.append((value[:8], value[8:]))
+        for first, item in enumerate(dft16(items)):
+            item = scale(item, first * chunk, 256)
+            mid_ref[first, chunk, 0] = item[0]
+            mid_ref[first, chunk, 1] = item[1]
+    for first in range(16):
+        items = [(mid_ref[first, chunk, 0], mid_ref[first, chunk, 1]) for chunk in range(16)]
+        for second, item in enumerate(dft16(items)):
+            at = first + 16 * second
+            cosine = cos_ref[at : at + 1, :]
+            sine = sin_ref[at : at + 1, :]
+            rows = pl.ds(at, 8, stride=GAP)
+            real_ref[rows, :] = item[0] * cosine - item[1] * sine
+            imag_ref[rows, :] = item[0] * sine + item[1] * cosine
     last_hi = last_hi_ref[...]
     last_lo = last_lo_ref[...]
-    cosine = cos_ref[...]
-    sine = sin_ref[...]
     for g in range(8):
-        x = jnp.concatenate(
-            [
-                get_ref[pl.ds(g, 256, stride=16), :].astype(BF16),
-                get_ref[pl.ds(8 + g, 256, stride=16), :].astype(BF16),
-            ],
-            axis=0,
-        )
-        mid = jnp.dot(first_hi, x, preferred_element_type=F32) + jnp.dot(
-            first_lo, x, preferred_element_type=F32
-        )
-        real, imag = mid[:256], mid[256:]
         both = jnp.concatenate(
-            [real * cosine - imag * sine, real * sine + imag * cosine], axis=1
+            [real_ref[g * GAP : g * GAP + 256, :], imag_ref[g * GAP : g * GAP + 256, :]], axis=1
         )
         high, low = split_value(both)
         made = nt_dot(last_hi, high) + nt_dot(last_lo, high) + nt_dot(last_hi, low)
@@ -320,7 +339,12 @@
     return pl.pallas_call(
         column_kernel,
         out_shape=jax.ShapeDtypeStruct((32, N), F32),
-        scratch_shapes=[pltpu.VMEM((4096, 128), F32), pltpu.VMEM((2048, 128), F32)],
+        scratch_shapes=[
+            pltpu.VMEM((16, 16, 2, 8, 128), F32),
+            pltpu.VMEM((8 * GAP, 128), F32),
+            pltpu.VMEM((8 * GAP, 128), F32),
+            pltpu.VMEM((2048, 128), F32),
+        ],
         compiler_params=pltpu.CompilerParams(vmem_limit_bytes=VMEM_LIMIT),
         name="column_transform",
     )(x, *tables)
@@ -332,16 +356,13 @@
     return row // BAND, col // BAND, row % BAND * BAND + col % BAND
 
 
-def send_ids(own_row, facet_id):
+def send_code(own_row):
     band, column, slot = block_of(own_row)
-    key = band * 16 + column
+    key = column * 16 + band
     number = jnp.arange(own_row.shape[0], dtype=jnp.int32)
-    same = (key[None, :] == key[:, None]) & (number[None, :] < number[:, None])
-    rank = jnp.sum(same.astype(jnp.int32), axis=1)
-    want_band = jnp.repeat(jnp.arange(16, dtype=jnp.int32), CAP)[:, None]
-    want_rank = jnp.tile(jnp.arange(CAP, dtype=jnp.int32), 16)[:, None]
-    hit = (key[None, :] == want_band * 16 + facet_id) & (rank[None, :] == want_rank)
-    return jnp.sum(jnp.where(hit, number[None, :], 0), axis=1)
+    same = (key[None, :] == key[:, None]) & (number[:, None] < number[None, :])
+    rank = jnp.sum(same.astype(jnp.int32), axis=0)
+    return (key * CAP + rank)[None, :]
 
 
 def receive_table(sub_index, my_band, my_column):
@@ -370,28 +391,20 @@
 def shards(visibilities, coordinates, phases, sub_index):
     facet_id = lax.axis_index("facet")
     span_id = lax.axis_index("span")
-    blocks = visibilities.shape[1]
     with jax.named_scope("rotate"):
-        vis = visibilities[0].reshape(blocks, 2, 8, 128).astype(F32)
-        place = coordinates[0].reshape(blocks, 16, 128)
-        angle = phases[0].reshape(blocks, 8, 128)
-        cosine = jnp.cos(angle)
-        sine = jnp.sin(angle)
-        real = vis[:, 0] * cosine - vis[:, 1] * sine
-        imag = vis[:, 0] * sine + vis[:, 1] * cosine
-        records = jnp.concatenate([real.astype(BF16), imag.astype(BF16), place], axis=1)
-    with jax.named_scope("gather_span"):
-        everything = lax.all_gather(records, "facet", axis=0, tiled=True)
+        parts = rotate_blocks(visibilities[0], coordinates[0], phases[0])
+    with jax.named_scope("spread_span"):
+        spread = lax.all_to_all(parts, "facet", split_axis=0, concat_axis=0, tiled=True)
     with jax.named_scope("choose"):
         own_row = lax.dynamic_index_in_dim(sub_index, span_id, 0, keepdims=False)
-        chosen = pick_blocks(send_ids(own_row, facet_id), everything)
+        chosen = pick_blocks(send_code(own_row), spread.reshape(-1, 256))
         order, slots, count = receive_table(sub_index, span_id, facet_id)
     with jax.named_scope("to_owner"):
         arrived = lax.all_to_all(
-            chosen.reshape(16, CAP, 32, 128), "span", split_axis=0, concat_axis=0, tiled=True
+            chosen, ("facet", "span"), split_axis=0, concat_axis=0, tiled=True
         )
     with jax.named_scope("gridding"):
-        block = grid_blocks(order, slots, count, arrived.reshape(16 * CAP, 32, 128))
+        block = grid_blocks(order, slots, count, arrived)
     with jax.named_scope("to_rows"):
         rows = lax.all_to_all(block, "facet", split_axis=0, concat_axis=0, tiled=True)
     with jax.named_scope("rows_dft"):

time: 217 us -> 144 us (0.66)
  waiting for transfers between devices: 72.5 us -> 25.4 us
  Pallas kernels: 43.8 us -> 24.7 us
  between operations: 13.5 us -> 0.09 us
  starting transfers between devices: 7.71 us -> 20.5 us
  blocking collectives: 68.3 us -> 65.5 us
  other arithmetic: 5.3 us -> 2.82 us
    all_gather x1 -> x0, waiting for transfers between devices: 57.7 us -> none  [shards(): everything = lax.all_gather(records, 'facet', axis=0, tiled=True)]
    pallas_call x1 -> x2, Pallas kernels: 17.7 us -> 4.82 us  [the longest x1 2.57 us: pick_blocks(): pl.pallas_call(pick_kernel, out_shape=jax.ShapeDtypeStruct((256, 8, 128),...]
    all_to_all x1 -> x2, starting transfers between devices: 7.71 us -> 20.5 us  [the longest x1 12.8 us: shards(): lax.all_to_all(chosen, ('facet', 'span'), split_axis=0, concat_axis=0, ti...]
    all_to_all x1 -> x2, waiting for transfers between devices: 14.8 us -> 25.4 us  [the longest x1 18.8 us: shards(): lax.all_to_all(chosen, ('facet', 'span'), split_axis=0, concat_axis=0, ti...]
    all_to_all x1, blocking collectives: 49.5 us -> 44.8 us  [shards(): lax.all_to_all(half_done, ('facet', 'span'), split_axis=0, concat_axis=0,...]
    pallas_call x1, Pallas kernels: 10.3 us -> 5.74 us  [column_transform(): pl.pallas_call(column_kernel, out_shape=jax.ShapeDtypeStruct((32, N), F32...]
where the time goes in v2:
time: 144 us; the launch traced here: 143 us
  blocking collectives  65.5 us (45%)
  waiting for transfers between devices  25.4 us (18%)
  Pallas kernels  24.7 us (17%)
  starting transfers between devices  20.5 us (14%)
  local copies, waits for them, and re-layouts  3.56 us (2%)
  other arithmetic  2.82 us (2%)
    all_to_all x1, blocking collectives, shards(): lax.all_to_all(half_done, ('facet', 'span'), split_axis=0, concat_axis=0,...  44.8 us
    all_to_all x1, blocking collectives, shards(): lax.all_to_all(block, 'facet', split_axis=0, concat_axis=0, tiled=True)  20.7 us
    all_to_all x1, waiting for transfers between devices, shards(): lax.all_to_all(chosen, ('facet', 'span'), split_axis=0, concat_axis=0, ti...  18.8 us
    all_to_all x1, starting transfers between devices, shards(): lax.all_to_all(chosen, ('facet', 'span'), split_axis=0, concat_axis=0, ti...  12.8 us
    pallas_call x1, Pallas kernels, grid_blocks(): pl.pallas_call(grid_kernel, out_shape=jax.ShapeDtypeStruct((16, 2, 32, 51...  8.86 us
    all_to_all x1, starting transfers between devices, shards(): lax.all_to_all(parts, 'facet', split_axis=0, concat_axis=0, tiled=True)  7.72 us
    all_to_all x1, waiting for transfers between devices, shards(): lax.all_to_all(parts, 'facet', split_axis=0, concat_axis=0, tiled=True)  6.61 us
    pallas_call x1, Pallas kernels, column_transform(): pl.pallas_call(column_kernel, out_shape=jax.ShapeDtypeStruct((32, N), F32...  5.74 us
  transfers between devices with their start and end apart: 2, of which 2 were waited for; matrix products, arithmetic and copies ran while one was open for 2% of the time, Pallas kernels for 0%

profile of v2, /device:TPU:1, one launch (start us, length us, event | category | flops | bytes accessed | tf_op | source)
XLA Modules:
  0.0 142.9 jit_solution(10735509003711557862)
XLA Ops:
  0.0 0.0 copy-start.3
  0.0 1.0 copy.24
  1.0 0.0 copy-done.3
  1.0 0.7 slice_bitcast_fusion
  1.7 2.2 %rotate_blocks.1 = bf16[16,32,256]{2,1,0:T(8,128)(2,1)} custom-call(bf16[32,1024]{1,0:T(8,128)(2,1)} %get-tuple-element.13.vis0_ref, bf16[32,1024]{1,0:T(8,128)(2,1)} %get-tuple-element.14.vis1_ref, bf16[32,1024]{1,0:T(8,128)(2,1)} %get-tuple-element.10.u_ref, bf16[32,1024]{1,0:T(8,128)(2,1)} %get-tuple-element.9.v_ref, f32[32,1024]{1,0:T(8,128)} %bitcast.24), custom_call_target="tpu_custom_call" | custom-call | tf_op jit(solution)/shard_map/rotate/rotate_blocks/pallas_call | solution.py:90
  4.0 0.0 copy-start.2
  4.0 7.7 %all-to-all-start = ((bf16[16,32,256]{2,1,0:T(8,128)(2,1)}), bf16[16,32,256]{2,1,0:T(8,128)(2,1)S(1)}, u32[]{:S(2)}, u32[]{:S(2)}) async-start(bf16[16,32,256]{2,1,0:T(8,128)(2,1)} %rotate_blocks.1), calls=%async_computation | async-start | bytes 524288 | tf_op jit(solution)/shard_map/spread_span/all_to_all | solution.py:397
  11.7 0.0 copy-done.2
  11.7 0.1 fusion.21
  11.8 0.2 convert_reduce_fusion
  12.0 0.6 multiply_add_fusion.code_ref
  12.5 6.6 %all-to-all-done = bf16[16,32,256]{2,1,0:T(8,128)(2,1)S(1)} async-done(((bf16[16,32,256]{2,1,0:T(8,128)(2,1)}), bf16[16,32,256]{2,1,0:T(8,128)(2,1)S(1)}, u32[]{:S(2)}, u32[]{:S(2)}) %all-to-all-start) | async-done | bytes 262176 | tf_op jit(solution)/shard_map/spread_span/all_to_all | solution.py:397
  19.1 0.0 copy-start.1
  19.2 0.7 copy-done.1
  19.8 2.6 %pick_blocks.1 = bf16[256,8,128]{2,1,0:T(8,128)(2,1)} custom-call(s32[1,512]{1,0:T(1,128)} %multiply_add_fusion.code_ref, bf16[512,256]{1,0:T(8,128)(2,1)} %bitcast.21), custom_call_target="tpu_custom_call" | custom-call | tf_op jit(solution)/shard_map/choose/pick_blocks/pallas_call | solution.py:116
  22.4 12.8 %all-to-all-start.1 = ((bf16[256,8,128]{2,1,0:T(8,128)(2,1)}), bf16[256,8,128]{2,1,0:T(8,128)(2,1)S(1)}, u32[]{:S(2)}, u32[]{:S(2)}) async-start(bf16[256,8,128]{2,1,0:T(8,128)(2,1)} %pick_blocks.1), calls=%async_computation.1 | async-start | bytes 1048576 | tf_op jit(solution)/shard_map/to_owner/all_to_all | solution.py:403
  35.2 0.1 fusion.13
  35.3 0.2 fusion.1
  35.4 0.2 fusion.3
  35.6 0.1 copy.17
  35.7 0.1 and.137
  35.8 0.1 fusion.7
  35.9 0.2 select_reduce_fusion
  36.0 0.1 copy.18
  36.1 0.1 broadcast_in_dim.49
  36.2 0.7 convert_reduce_fusion.2
  36.9 0.1 convert_reduce_fusion.1
  37.0 0.7 select_reduce_fusion.1
  37.8 18.8 %all-to-all-done.1.vis_ref = bf16[256,8,128]{2,1,0:T(8,128)(2,1)S(1)} async-done(((bf16[256,8,128]{2,1,0:T(8,128)(2,1)}), bf16[256,8,128]{2,1,0:T(8,128)(2,1)S(1)}, u32[]{:S(2)}, u32[]{:S(2)}) %all-to-all-start.1) | async-done | bytes 524320 | tf_op jit(solution)/shard_map/to_owner/all_to_all | solution.py:403
  56.6 0.0 copy-start
  56.6 0.8 copy-done
  57.4 8.9 %grid_blocks.1 = bf16[16,2,32,512]{3,2,1,0:T(8,128)(2,1)} custom-call(s32[64]{0:T(128)} %get-tuple-element.6.order_ref, s32[64]{0:T(128)} %get-tuple-element.5.slot_ref, s32[1]{0:T(128)} %bitcast.count_ref, bf16[256,8,128]{2,1,0:T(8,128)(2,1)} %copy-done), custom_call_target="tpu_custom_call" | custom-call | tf_op jit(solution)/shard_map/gridding/grid_blocks/pallas_call | solution.py:173
  66.3 20.7 %all_to_all.20.x_ref = bf16[16,2,32,512]{3,2,1,0:T(8,128)(2,1)} all-to-all(bf16[16,2,32,512]{3,2,1,0:T(8,128)(2,1)} %grid_blocks.1), channel_id=1, replica_groups=mesh['facet'=16,'span'=16] {'facet'}, dimensions={0} | all-to-all | bytes 2097152 | tf_op jit(solution)/shard_map/to_rows/all_to_all | solution.py:409
  87.0 5.3 %row_transform.1 = bf16[256,16,128]{2,1,0:T(8,128)(2,1)} custom-call(bf16[16,2,32,512]{3,2,1,0:T(8,128)(2,1)} %all_to_all.20.x_ref, bf16[256,256]{1,0:T(8,128)(2,1)} %constant.127.clone.dft_hi_ref, bf16[256,256]{1,0:T(8,128)(2,1)} %constant.128.clone.dft_lo_ref, f32[64,128]{1,0:T(8,128)} %constant.129.clone.cos_ref, f32[64,128]{1,0:T(8,128)} %constant.130.clone.sin_ref), custom_call_target="tpu_custom_call" | custom-call | tf_op jit(solution)/shard_map/rows_dft/row_transform/pallas_call | solution.py:283
  92.3 44.8 %all_to_all.21.x_ref = bf16[256,16,128]{2,1,0:T(8,128)(2,1)} all-to-all(bf16[256,16,128]{2,1,0:T(8,128)(2,1)} %row_transform.1), channel_id=1, replica_groups=mesh['facet'=16,'span'=16] {'facet','span'}, dimensions={0} | all-to-all | bytes 2097152 | tf_op jit(solution)/shard_map/to_columns/all_to_all | solution.py:413
  137.1 5.7 %column_transform.1 = f32[32,8192]{1,0:T(8,128)} custom-call(bf16[256,16,128]{2,1,0:T(8,128)(2,1)} %all_to_all.21.x_ref, f32[256,128]{1,0:T(8,128)} %constant.131.clone.cos_ref, f32[256,128]{1,0:T(8,128)} %constant.132.clone.sin_ref, bf16[128,256]{1,0:T(8,128)(2,1)} %constant.133.clone.last_hi_ref, bf16[128,256]{1,0:T(8,128)(2,1)} %constant.134.clone.last_lo_ref), custom_call_target="tpu_custom_call" | custom-call | tf_op jit(solution)/shard_map/columns_dft/column_transform/pallas_call | solution.py:339
  (2 shorter events, 0.0 us)
Async XLA Ops:
  0.0 1.0 copy-start.3
  4.0 7.7 %copy-start.2 = (s32[16,512]{1,0:T(8,128)S(1)}, s32[16,512]{1,0:T(8,128)}, u32[]{:S(2)}) copy-start(s32[16,512]{1,0:T(8,128)} %param.15) | copy-start | bytes 98308
  4.0 15.2 %all-to-all-start = ((bf16[16,32,256]{2,1,0:T(8,128)(2,1)}), bf16[16,32,256]{2,1,0:T(8,128)(2,1)S(1)}, u32[]{:S(2)}, u32[]{:S(2)}) async-start(bf16[16,32,256]{2,1,0:T(8,128)(2,1)} %rotate_blocks.1), calls=%async_computation | async-start | bytes 524288 | tf_op jit(solution)/shard_map/spread_span/all_to_all | solution.py:397
  19.1 0.7 copy-start.1
  22.4 34.2 %all-to-all-start.1 = ((bf16[256,8,128]{2,1,0:T(8,128)(2,1)}), bf16[256,8,128]{2,1,0:T(8,128)(2,1)S(1)}, u32[]{:S(2)}, u32[]{:S(2)}) async-start(bf16[256,8,128]{2,1,0:T(8,128)(2,1)} %pick_blocks.1), calls=%async_computation.1 | async-start | bytes 1048576 | tf_op jit(solution)/shard_map/to_owner/all_to_all | solution.py:403
  56.6 0.8 copy-start

commit v3 on v2

--- a/solution.py
+++ b/solution.py
@@ -17,7 +17,8 @@
 F32 = jnp.float32
 BF16 = jnp.bfloat16
 GAUSS = -1.0 / (2.0 * SPREAD * SPREAD * np.log(2.0))
-VMEM_LIMIT = 56 * 1024 * 1024
+VMEM_LIMIT = 24 * 1024 * 1024
+LOCAL = pl.BlockSpec(memory_space=pltpu.VMEM)
 
 
 def angle_tables(rows, cols, length):
@@ -90,6 +91,8 @@
     return pl.pallas_call(
         rotate_kernel,
         out_shape=jax.ShapeDtypeStruct((16, blocks, 256), BF16),
+        in_specs=[LOCAL] * 5,
+        out_specs=LOCAL,
         name="rotate_blocks",
     )(
         visibilities[:, 0],
@@ -116,6 +119,8 @@
     return pl.pallas_call(
         pick_kernel,
         out_shape=jax.ShapeDtypeStruct((256, 8, 128), BF16),
+        in_specs=[LOCAL] * 2,
+        out_specs=LOCAL,
         scratch_shapes=[pltpu.VMEM((2048, 128), F32)],
         compiler_params=pltpu.CompilerParams(vmem_limit_bytes=VMEM_LIMIT),
         name="pick_blocks",
@@ -169,20 +174,15 @@
 
 
 def grid_blocks(order, slots, count, vis):
-    whole = lambda *_: (0, 0, 0)
     return pl.pallas_call(
         grid_kernel,
         out_shape=jax.ShapeDtypeStruct((16, 2, 32, 512), BF16),
-        grid_spec=pltpu.PrefetchScalarGridSpec(
-            num_scalar_prefetch=3,
-            grid=(1,),
-            in_specs=[pl.BlockSpec(vis.shape, whole)],
-            out_specs=pl.BlockSpec((16, 2, 32, 512), lambda *_: (0, 0, 0, 0)),
-            scratch_shapes=[
-                pltpu.VMEM((2048, 128), F32),
-                pltpu.VMEM((BAND * BAND, 2 * P_SIZE, P_SIZE), F32),
-            ],
-        ),
+        in_specs=[pl.BlockSpec(memory_space=pltpu.SMEM)] * 3 + [LOCAL],
+        out_specs=LOCAL,
+        scratch_shapes=[
+            pltpu.VMEM((2048, 128), F32),
+            pltpu.VMEM((BAND * BAND, 2 * P_SIZE, P_SIZE), F32),
+        ],
         compiler_params=pltpu.CompilerParams(vmem_limit_bytes=VMEM_LIMIT),
         name="grid_blocks",
     )(order, slots, count, vis)
@@ -283,6 +283,8 @@
     return pl.pallas_call(
         row_kernel,
         out_shape=jax.ShapeDtypeStruct((256, 16, 128), BF16),
+        in_specs=[LOCAL] * (1 + len(tables)),
+        out_specs=LOCAL,
         scratch_shapes=[
             pltpu.VMEM((4, 16, 2, 32, 128), F32),
             pltpu.VMEM((2048, 256), BF16),
@@ -339,6 +341,8 @@
     return pl.pallas_call(
         column_kernel,
         out_shape=jax.ShapeDtypeStruct((32, N), F32),
+        in_specs=[LOCAL] * (1 + len(tables)),
+        out_specs=LOCAL,
         scratch_shapes=[
             pltpu.VMEM((16, 16, 2, 8, 128), F32),
             pltpu.VMEM((8 * GAP, 128), F32),

time: 144 us -> 135 us (0.938)
  Pallas kernels: 24.7 us -> 16.3 us
  blocking collectives: 65.5 us -> 67.3 us
    pallas_call x1, Pallas kernels: 8.86 us -> 5.04 us  [grid_blocks(): pl.pallas_call(grid_kernel, out_shape=jax.ShapeDtypeStruct((16, 2, 32, 51...]
    pallas_call x1, Pallas kernels: 5.33 us -> 3.03 us  [row_transform(): pl.pallas_call(row_kernel, out_shape=jax.ShapeDtypeStruct((256, 16, 128),...]
    all_to_all x1, blocking collectives: 44.8 us -> 46.3 us  [shards(): lax.all_to_all(half_done, ('facet', 'span'), split_axis=0, concat_axis=0,...]
where the time goes in v3:
time: 135 us
  blocking collectives  67.3 us (50%)
  waiting for transfers between devices  26.6 us (20%)
  starting transfers between devices  20.5 us (15%)
  Pallas kernels  16.3 us (12%)
  local copies, waits for them, and re-layouts  2.13 us (2%)
  other arithmetic  1.66 us (1%)
    all_to_all x1, blocking collectives, shards(): lax.all_to_all(half_done, ('facet', 'span'), split_axis=0, concat_axis=0,...  46.3 us
    all_to_all x1, blocking collectives, shards(): lax.all_to_all(block, 'facet', split_axis=0, concat_axis=0, tiled=True)  21 us
    all_to_all x1, waiting for transfers between devices, shards(): lax.all_to_all(chosen, ('facet', 'span'), split_axis=0, concat_axis=0, ti...  19.4 us
    all_to_all x1, starting transfers between devices, shards(): lax.all_to_all(chosen, ('facet', 'span'), split_axis=0, concat_axis=0, ti...  12.8 us
    all_to_all x1, starting transfers between devices, shards(): lax.all_to_all(parts, 'facet', split_axis=0, concat_axis=0, tiled=True)  7.72 us
    all_to_all x1, waiting for transfers between devices, shards(): lax.all_to_all(parts, 'facet', split_axis=0, concat_axis=0, tiled=True)  7.17 us
    pallas_call x1, Pallas kernels, grid_blocks(): pl.pallas_call(grid_kernel, out_shape=jax.ShapeDtypeStruct((16, 2, 32, 51...  5.04 us
    pallas_call x1, Pallas kernels, column_transform(): pl.pallas_call(column_kernel, out_shape=jax.ShapeDtypeStruct((32, N), F32...  4.4 us
  transfers between devices with their start and end apart: 2, of which 2 were waited for; matrix products, arithmetic and copies ran while one was open for 2% of the time, Pallas kernels for 0%

profile of v3, /device:TPU:1, one launch (start us, length us, event | category | flops | bytes accessed | tf_op | source)
XLA Modules:
  0.0 134.9 jit_solution(2464715664077574781)
XLA Ops:
  0.0 0.0 copy-start.9
  0.0 1.0 copy.24
  1.0 0.0 copy-done.9
  1.0 0.7 slice_bitcast_fusion
  1.7 2.2 %rotate_blocks.1 = bf16[16,32,256]{2,1,0:T(8,128)(2,1)} custom-call(bf16[32,1024]{1,0:T(8,128)(2,1)} %get-tuple-element.13.vis0_ref, bf16[32,1024]{1,0:T(8,128)(2,1)} %get-tuple-element.14.vis1_ref, bf16[32,1024]{1,0:T(8,128)(2,1)} %get-tuple-element.10.u_ref, bf16[32,1024]{1,0:T(8,128)(2,1)} %get-tuple-element.9.v_ref, f32[32,1024]{1,0:T(8,128)} %bitcast.24), custom_call_target="tpu_custom_call" | custom-call | tf_op jit(solution)/shard_map/rotate/rotate_blocks/pallas_call | solution.py:91
  4.0 0.0 copy-start.8
  4.0 7.7 %all-to-all-start = ((bf16[16,32,256]{2,1,0:T(8,128)(2,1)}), bf16[16,32,256]{2,1,0:T(8,128)(2,1)S(1)}, u32[]{:S(2)}, u32[]{:S(2)}) async-start(bf16[16,32,256]{2,1,0:T(8,128)(2,1)} %rotate_blocks.1), calls=%async_computation | async-start | bytes 524288 | tf_op jit(solution)/shard_map/spread_span/all_to_all | solution.py:401
  11.7 0.0 copy-done.8
  11.7 0.1 fusion.21
  11.8 0.2 convert_reduce_fusion
  12.0 7.2 %all-to-all-done = bf16[16,32,256]{2,1,0:T(8,128)(2,1)S(1)} async-done(((bf16[16,32,256]{2,1,0:T(8,128)(2,1)}), bf16[16,32,256]{2,1,0:T(8,128)(2,1)S(1)}, u32[]{:S(2)}, u32[]{:S(2)}) %all-to-all-start) | async-done | bytes 262176 | tf_op jit(solution)/shard_map/spread_span/all_to_all | solution.py:401
  19.1 1.6 %pick_blocks.1 = bf16[256,8,128]{2,1,0:T(8,128)(2,1)} custom-call(s32[1,512]{1,0:T(1,128)S(1)} %multiply_add_fusion.code_ref, bf16[512,256]{1,0:T(8,128)(2,1)S(1)} %bitcast.21), custom_call_target="tpu_custom_call" | custom-call | tf_op jit(solution)/shard_map/choose/pick_blocks/pallas_call | solution.py:119
  20.8 12.8 %all-to-all-start.1 = ((bf16[256,8,128]{2,1,0:T(8,128)(2,1)}), bf16[256,8,128]{2,1,0:T(8,128)(2,1)S(1)}, u32[]{:S(2)}, u32[]{:S(2)}) async-start(bf16[256,8,128]{2,1,0:T(8,128)(2,1)} %pick_blocks.1), calls=%async_computation.1 | async-start | bytes 1048576 | tf_op jit(solution)/shard_map/to_owner/all_to_all | solution.py:407
  33.5 0.1 fusion.13
  33.6 0.2 fusion.1
  33.8 0.2 fusion.3
  34.0 0.1 copy.17
  34.1 0.1 and.137
  34.2 0.1 fusion.7
  34.2 0.2 select_reduce_fusion
  34.4 0.1 copy.18
  34.5 0.1 broadcast_in_dim.49
  34.6 0.7 convert_reduce_fusion.2
  35.3 0.1 convert_reduce_fusion.1
  35.4 0.1 select_reduce_fusion.1
  35.5 19.4 %all-to-all-done.1.vis_ref = bf16[256,8,128]{2,1,0:T(8,128)(2,1)S(1)} async-done(((bf16[256,8,128]{2,1,0:T(8,128)(2,1)}), bf16[256,8,128]{2,1,0:T(8,128)(2,1)S(1)}, u32[]{:S(2)}, u32[]{:S(2)}) %all-to-all-start.1) | async-done | bytes 524320 | tf_op jit(solution)/shard_map/to_owner/all_to_all | solution.py:407
  55.0 5.0 %grid_blocks.1 = bf16[16,2,32,512]{3,2,1,0:T(8,128)(2,1)S(1)} custom-call(s32[64]{0:T(128)S(1)} %get-tuple-element.6.order_ref, s32[64]{0:T(128)S(1)} %get-tuple-element.5.slot_ref, s32[1]{0:T(128)} %bitcast.count_ref, bf16[256,8,128]{2,1,0:T(8,128)(2,1)S(1)} %all-to-all-done.1.vis_ref), custom_call_target="tpu_custom_call" | custom-call | tf_op jit(solution)/shard_map/gridding/grid_blocks/pallas_call | solution.py:177
  60.0 0.0 copy-start.2
  60.0 0.0 copy-start.3
  60.0 0.0 copy-start.6
  60.0 0.0 copy-start.7
  60.1 21.0 %all_to_all.20.x_ref = bf16[16,2,32,512]{3,2,1,0:T(8,128)(2,1)S(1)} all-to-all(bf16[16,2,32,512]{3,2,1,0:T(8,128)(2,1)S(1)} %grid_blocks.1), channel_id=1, replica_groups=mesh['facet'=16,'span'=16] {'facet'}, dimensions={0} | all-to-all | bytes 2097152 | tf_op jit(solution)/shard_map/to_rows/all_to_all | solution.py:413
  81.0 0.0 copy-done.2
  81.0 0.0 copy-done.3
  81.0 0.0 copy-done.6
  81.1 0.0 copy-done.7
  81.1 3.0 %row_transform.1 = bf16[256,16,128]{2,1,0:T(8,128)(2,1)S(1)} custom-call(bf16[16,2,32,512]{3,2,1,0:T(8,128)(2,1)S(1)} %all_to_all.20.x_ref, bf16[256,256]{1,0:T(8,128)(2,1)S(1)} %copy-done.3, bf16[256,256]{1,0:T(8,128)(2,1)S(1)} %copy-done.2, f32[64,128]{1,0:T(8,128)S(1)} %copy-done.7, f32[64,128]{1,0:T(8,128)S(1)} %copy-done.6), custom_call_target="tpu_custom_call" | custom-call | tf_op jit(solution)/shard_map/rows_dft/row_transform/pallas_call | solution.py:283
  84.1 0.0 copy-start
  84.1 0.0 copy-start.1
  84.1 0.0 copy-start.4
  84.1 0.0 copy-start.5
  84.2 46.3 %all_to_all.21.x_ref = bf16[256,16,128]{2,1,0:T(8,128)(2,1)S(1)} all-to-all(bf16[256,16,128]{2,1,0:T(8,128)(2,1)S(1)} %row_transform.1), channel_id=1, replica_groups=mesh['facet'=16,'span'=16] {'facet','span'}, dimensions={0} | all-to-all | bytes 2097152 | tf_op jit(solution)/shard_map/to_columns/all_to_all | solution.py:417
  130.4 0.0 copy-done
  130.4 0.0 copy-done.1
  130.4 0.0 copy-done.4
  130.4 0.0 copy-done.5
  130.5 4.4 %column_transform.1 = f32[32,8192]{1,0:T(8,128)} custom-call(bf16[256,16,128]{2,1,0:T(8,128)(2,1)S(1)} %all_to_all.21.x_ref, f32[256,128]{1,0:T(8,128)S(1)} %copy-done.1, f32[256,128]{1,0:T(8,128)S(1)} %copy-done, bf16[128,256]{1,0:T(8,128)(2,1)S(1)} %copy-done.5, bf16[128,256]{1,0:T(8,128)(2,1)S(1)} %copy-done.4), custom_call_target="tpu_custom_call" | custom-call | tf_op jit(solution)/shard_map/columns_dft/column_transform/pallas_call | solution.py:341
  (3 shorter events, 0.1 us)
Async XLA Ops:
  0.0 1.0 copy-start.9
  4.0 7.7 %copy-start.8 = (s32[16,512]{1,0:T(8,128)S(1)}, s32[16,512]{1,0:T(8,128)}, u32[]{:S(2)}) copy-start(s32[16,512]{1,0:T(8,128)} %param.15) | copy-start | bytes 98308
  4.0 15.2 %all-to-all-start = ((bf16[16,32,256]{2,1,0:T(8,128)(2,1)}), bf16[16,32,256]{2,1,0:T(8,128)(2,1)S(1)}, u32[]{:S(2)}, u32[]{:S(2)}) async-start(bf16[16,32,256]{2,1,0:T(8,128)(2,1)} %rotate_blocks.1), calls=%async_computation | async-start | bytes 524288 | tf_op jit(solution)/shard_map/spread_span/all_to_all | solution.py:401
  20.8 34.2 %all-to-all-start.1 = ((bf16[256,8,128]{2,1,0:T(8,128)(2,1)}), bf16[256,8,128]{2,1,0:T(8,128)(2,1)S(1)}, u32[]{:S(2)}, u32[]{:S(2)}) async-start(bf16[256,8,128]{2,1,0:T(8,128)(2,1)} %pick_blocks.1), calls=%async_computation.1 | async-start | bytes 1048576 | tf_op jit(solution)/shard_map/to_owner/all_to_all | solution.py:407
  60.0 21.0 %copy-start.2 = (bf16[256,256]{1,0:T(8,128)(2,1)S(1)}, bf16[256,256]{1,0:T(8,128)(2,1)}, u32[]{:S(2)}) copy-start(bf16[256,256]{1,0:T(8,128)(2,1)} %constant.128.clone.dft_lo_ref) | copy-start | bytes 393220
  60.0 21.0 %copy-start.3 = (bf16[256,256]{1,0:T(8,128)(2,1)S(1)}, bf16[256,256]{1,0:T(8,128)(2,1)}, u32[]{:S(2)}) copy-start(bf16[256,256]{1,0:T(8,128)(2,1)} %constant.127.clone.dft_hi_ref) | copy-start | bytes 393220
  60.0 21.0 %copy-start.6 = (f32[64,128]{1,0:T(8,128)S(1)}, f32[64,128]{1,0:T(8,128)}, u32[]{:S(2)}) copy-start(f32[64,128]{1,0:T(8,128)} %constant.130.clone.sin_ref) | copy-start | bytes 98308
  60.0 21.0 %copy-start.7 = (f32[64,128]{1,0:T(8,128)S(1)}, f32[64,128]{1,0:T(8,128)}, u32[]{:S(2)}) copy-start(f32[64,128]{1,0:T(8,128)} %constant.129.clone.cos_ref) | copy-start | bytes 98308
  84.1 46.3 %copy-start = (f32[256,128]{1,0:T(8,128)S(1)}, f32[256,128]{1,0:T(8,128)}, u32[]{:S(2)}) copy-start(f32[256,128]{1,0:T(8,128)} %constant.132.clone.sin_ref) | copy-start | bytes 393220
  84.1 46.3 %copy-start.1 = (f32[256,128]{1,0:T(8,128)S(1)}, f32[256,128]{1,0:T(8,128)}, u32[]{:S(2)}) copy-start(f32[256,128]{1,0:T(8,128)} %constant.131.clone.cos_ref) | copy-start | bytes 393220
  84.1 46.3 %copy-start.4 = (bf16[128,256]{1,0:T(8,128)(2,1)S(1)}, bf16[128,256]{1,0:T(8,128)(2,1)}, u32[]{:S(2)}) copy-start(bf16[128,256]{1,0:T(8,128)(2,1)} %constant.134.clone.last_lo_ref) | copy-start | bytes 196612
  84.1 46.3 %copy-start.5 = (bf16[128,256]{1,0:T(8,128)(2,1)S(1)}, bf16[128,256]{1,0:T(8,128)(2,1)}, u32[]{:S(2)}) copy-start(bf16[128,256]{1,0:T(8,128)(2,1)} %constant.133.clone.last_hi_ref) | copy-start | bytes 196612

commit v4 on v3

--- a/solution.py
+++ b/solution.py
@@ -11,6 +11,8 @@
 CAP = 4
 STEP = 8
 GAP = 264
+PAD = 40
+WIDE = 136
 SIDE = N // P_SIZE
 BAND = 4
 SPREAD = 0.75
@@ -72,18 +74,29 @@
     )
 
 
-def rotate_kernel(vis0_ref, vis1_ref, u_ref, v_ref, phase_ref, out_ref):
+def cos_sin(angle):
+    half = angle * 0.5
+    square = half * half
+    sine = jnp.full_like(half, 1.0 / 6227020800.0)
+    for coefficient in (-39916800.0, 362880.0, -5040.0, 120.0, -6.0, 1.0):
+        sine = sine * square + 1.0 / coefficient
+    sine = sine * half
+    cosine = jnp.full_like(half, 1.0 / 479001600.0)
+    for coefficient in (-3628800.0, 40320.0, -720.0, 24.0, -2.0, 1.0):
+        cosine = cosine * square + 1.0 / coefficient
+    return 1.0 - 2.0 * sine * sine, 2.0 * sine * cosine
+
+
+def rotate_kernel(vis_ref, place_ref, phase_ref, out_ref):
     for k in range(8):
         lanes = pl.ds(128 * k, 128)
-        phase = phase_ref[:, lanes]
-        cosine = jnp.cos(phase)
-        sine = jnp.sin(phase)
-        real = vis0_ref[:, lanes].astype(F32)
-        imag = vis1_ref[:, lanes].astype(F32)
+        cosine, sine = cos_sin(phase_ref[:, lanes])
+        real = vis_ref[:, 0, lanes].astype(F32)
+        imag = vis_ref[:, 1, lanes].astype(F32)
         out_ref[2 * k, :, :128] = (real * cosine - imag * sine).astype(BF16)
         out_ref[2 * k, :, 128:] = (real * sine + imag * cosine).astype(BF16)
-        out_ref[2 * k + 1, :, :128] = u_ref[:, lanes]
-        out_ref[2 * k + 1, :, 128:] = v_ref[:, lanes]
+        out_ref[2 * k + 1, :, :128] = place_ref[:, 0, lanes]
+        out_ref[2 * k + 1, :, 128:] = place_ref[:, 1, lanes]
 
 
 def rotate_blocks(visibilities, coordinates, phases):
@@ -91,16 +104,10 @@
     return pl.pallas_call(
         rotate_kernel,
         out_shape=jax.ShapeDtypeStruct((16, blocks, 256), BF16),
-        in_specs=[LOCAL] * 5,
+        in_specs=[LOCAL] * 3,
         out_specs=LOCAL,
         name="rotate_blocks",
-    )(
-        visibilities[:, 0],
-        visibilities[:, 1],
-        coordinates[:, 0],
-        coordinates[:, 1],
-        phases,
-    )
+    )(visibilities, coordinates, phases)
 
 
 def pick_kernel(code_ref, rows_ref, out_ref, put_ref):
@@ -129,7 +136,10 @@
 
 def grid_kernel(order_ref, slot_ref, count_ref, vis_ref, out_ref, wide_ref, acc_ref):
     acc_ref[...] = jnp.zeros_like(acc_ref)
-    wide_ref[...] = vis_ref[...].astype(F32).reshape(2048, 128)
+    for piece in range(16):
+        wide_ref[piece * WIDE : piece * WIDE + 128, :] = (
+            vis_ref[piece * 16 : (piece + 1) * 16].astype(F32).reshape(128, 128)
+        )
     cells = lax.broadcasted_iota(jnp.int32, (P_SIZE, 128), 0).astype(F32)
     count = count_ref[0]
 
@@ -137,8 +147,8 @@
         entry = order_ref[at]
         slot = slot_ref[at]
         keep = jnp.where(live, 1.0, 0.0).astype(F32)
-        first = wide_ref[pl.ds(2 * entry, 16, stride=128), :]
-        second = wide_ref[pl.ds(2 * entry + 1, 16, stride=128), :]
+        first = wide_ref[pl.ds(2 * entry, 16, stride=WIDE), :]
+        second = wide_ref[pl.ds(2 * entry + 1, 16, stride=WIDE), :]
         total = None
         for pair in range(4):
             left = []
@@ -180,7 +190,7 @@
         in_specs=[pl.BlockSpec(memory_space=pltpu.SMEM)] * 3 + [LOCAL],
         out_specs=LOCAL,
         scratch_shapes=[
-            pltpu.VMEM((2048, 128), F32),
+            pltpu.VMEM((16 * WIDE, 128), F32),
             pltpu.VMEM((BAND * BAND, 2 * P_SIZE, P_SIZE), F32),
         ],
         compiler_params=pltpu.CompilerParams(vmem_limit_bytes=VMEM_LIMIT),
@@ -272,10 +282,11 @@
         for part in range(2):
             for piece in range(2):
                 half, i = divmod(2 * n + piece, 8)
-                put_ref[pl.ds(half * 16 + part * 8 + i, 128, stride=32), :] = made[
+                put_ref[pl.ds(half * 16 + part * 8 + i, 128, stride=PAD), :] = made[
                     part * 128 : (part + 1) * 128, piece * 128 : (piece + 1) * 128
                 ]
-    out_ref[...] = put_ref[...].reshape(256, 16, 128).astype(BF16)
+    chunks = put_ref[...].reshape(128, PAD, 128)[:, :32]
+    out_ref[...] = chunks.reshape(256, 16, 128).astype(BF16)
 
 
 def row_transform(x):
@@ -289,7 +300,7 @@
             pltpu.VMEM((4, 16, 2, 32, 128), F32),
             pltpu.VMEM((2048, 256), BF16),
             pltpu.VMEM((2048, 256), BF16),
-            pltpu.VMEM((4096, 128), F32),
+            pltpu.VMEM((128 * PAD, 128), F32),
         ],
         compiler_params=pltpu.CompilerParams(vmem_limit_bytes=VMEM_LIMIT),
         name="row_transform",
@@ -326,13 +337,16 @@
         high, low = split_value(both)
         made = nt_dot(last_hi, high) + nt_dot(last_lo, high) + nt_dot(last_hi, low)
         for side in range(2):
-            start = side * 1024 + g * 128
-            put_ref[start : start + 128, :] = made[:, side * 128 : (side + 1) * 128]
+            for m in range(4):
+                start = (side * 32 + 4 * g + m) * PAD
+                put_ref[start : start + 32, :] = made[
+                    32 * m : 32 * m + 32, side * 128 : (side + 1) * 128
+                ]
     for gamma in range(32):
         for side in range(2):
             start = gamma * 256 + side * 128
             out_ref[:, start : start + 128] = put_ref[
-                pl.ds(side * 1024 + gamma, 32, stride=32), :
+                pl.ds(side * 32 * PAD + gamma, 32, stride=PAD), :
             ]
 
 
@@ -347,7 +361,7 @@
             pltpu.VMEM((16, 16, 2, 8, 128), F32),
             pltpu.VMEM((8 * GAP, 128), F32),
             pltpu.VMEM((8 * GAP, 128), F32),
-            pltpu.VMEM((2048, 128), F32),
+            pltpu.VMEM((64 * PAD, 128), F32),
         ],
         compiler_params=pltpu.CompilerParams(vmem_limit_bytes=VMEM_LIMIT),
         name="column_transform",

time: 135 us -> 131 us (0.970)
  local copies, waits for them, and re-layouts: 2.13 us -> 0.44 us
where the time goes in v4:
time: 131 us
  blocking collectives  66.8 us (51%)
  waiting for transfers between devices  26.6 us (20%)
  starting transfers between devices  20.5 us (16%)
  Pallas kernels  15 us (11%)
  other arithmetic  1.66 us (1%)
    all_to_all x1, blocking collectives, shards(): lax.all_to_all(half_done, ('facet', 'span'), split_axis=0, concat_axis=0,...  45.6 us
    all_to_all x1, blocking collectives, shards(): lax.all_to_all(block, 'facet', split_axis=0, concat_axis=0, tiled=True)  21.2 us
    all_to_all x1, waiting for transfers between devices, shards(): lax.all_to_all(chosen, ('facet', 'span'), split_axis=0, concat_axis=0, ti...  19.4 us
    all_to_all x1, starting transfers between devices, shards(): lax.all_to_all(chosen, ('facet', 'span'), split_axis=0, concat_axis=0, ti...  12.8 us
    all_to_all x1, starting transfers between devices, shards(): lax.all_to_all(parts, 'facet', split_axis=0, concat_axis=0, tiled=True)  7.72 us
    all_to_all x1, waiting for transfers between devices, shards(): lax.all_to_all(parts, 'facet', split_axis=0, concat_axis=0, tiled=True)  7.17 us
    pallas_call x1, Pallas kernels, grid_blocks(): pl.pallas_call(grid_kernel, out_shape=jax.ShapeDtypeStruct((16, 2, 32, 51...  4.97 us
    pallas_call x1, Pallas kernels, column_transform(): pl.pallas_call(column_kernel, out_shape=jax.ShapeDtypeStruct((32, N), F32...  3.87 us
  transfers between devices with their start and end apart: 2, of which 2 were waited for; matrix products, arithmetic and copies ran while one was open for 2% of the time, Pallas kernels for 0%

profile of v4, /device:TPU:1, one launch (start us, length us, event | category | flops | bytes accessed | tf_op | source)
XLA Modules:
  0.0 131.2 jit_solution(6272362087323765778)
XLA Ops:
  0.0 2.4 %rotate_blocks.1 = bf16[16,32,256]{2,1,0:T(8,128)(2,1)} custom-call(bf16[32,2,1024]{2,1,0:T(2,128)(2,1)} %bitcast.10, bf16[32,2,1024]{2,1,0:T(2,128)(2,1)} %bitcast.11, f32[32,1024]{1,0:T(8,128)} %bitcast.12), custom_call_target="tpu_custom_call" | custom-call | tf_op jit(solution)/shard_map/rotate/rotate_blocks/pallas_call | solution.py:104
  2.4 0.0 copy-start.8
  2.4 7.7 %all-to-all-start = ((bf16[16,32,256]{2,1,0:T(8,128)(2,1)}), bf16[16,32,256]{2,1,0:T(8,128)(2,1)S(1)}, u32[]{:S(2)}, u32[]{:S(2)}) async-start(bf16[16,32,256]{2,1,0:T(8,128)(2,1)} %rotate_blocks.1), calls=%async_computation | async-start | bytes 524288 | tf_op jit(solution)/shard_map/spread_span/all_to_all | solution.py:415
  10.2 0.0 copy-done.8
  10.2 0.1 fusion.21
  10.3 0.2 convert_reduce_fusion
  10.4 7.2 %all-to-all-done = bf16[16,32,256]{2,1,0:T(8,128)(2,1)S(1)} async-done(((bf16[16,32,256]{2,1,0:T(8,128)(2,1)}), bf16[16,32,256]{2,1,0:T(8,128)(2,1)S(1)}, u32[]{:S(2)}, u32[]{:S(2)}) %all-to-all-start) | async-done | bytes 262176 | tf_op jit(solution)/shard_map/spread_span/all_to_all | solution.py:415
  17.6 1.6 %pick_blocks.1 = bf16[256,8,128]{2,1,0:T(8,128)(2,1)} custom-call(s32[1,512]{1,0:T(1,128)S(1)} %multiply_add_fusion.code_ref, bf16[512,256]{1,0:T(8,128)(2,1)S(1)} %bitcast.9), custom_call_target="tpu_custom_call" | custom-call | tf_op jit(solution)/shard_map/choose/pick_blocks/pallas_call | solution.py:126
  19.2 12.8 %all-to-all-start.1 = ((bf16[256,8,128]{2,1,0:T(8,128)(2,1)}), bf16[256,8,128]{2,1,0:T(8,128)(2,1)S(1)}, u32[]{:S(2)}, u32[]{:S(2)}) async-start(bf16[256,8,128]{2,1,0:T(8,128)(2,1)} %pick_blocks.1), calls=%async_computation.1 | async-start | bytes 1048576 | tf_op jit(solution)/shard_map/to_owner/all_to_all | solution.py:421
  32.0 0.1 fusion.13
  32.1 0.2 fusion.1
  32.3 0.2 fusion.3
  32.4 0.1 copy.13
  32.5 0.1 and.137
  32.6 0.1 fusion.7
  32.7 0.2 select_reduce_fusion
  32.9 0.1 copy.14
  33.0 0.1 broadcast_in_dim.49
  33.1 0.7 convert_reduce_fusion.2
  33.8 0.1 convert_reduce_fusion.1
  33.9 0.1 select_reduce_fusion.1
  34.0 19.4 %all-to-all-done.1.vis_ref = bf16[256,8,128]{2,1,0:T(8,128)(2,1)S(1)} async-done(((bf16[256,8,128]{2,1,0:T(8,128)(2,1)}), bf16[256,8,128]{2,1,0:T(8,128)(2,1)S(1)}, u32[]{:S(2)}, u32[]{:S(2)}) %all-to-all-start.1) | async-done | bytes 524320 | tf_op jit(solution)/shard_map/to_owner/all_to_all | solution.py:421
  53.4 5.0 %grid_blocks.1 = bf16[16,2,32,512]{3,2,1,0:T(8,128)(2,1)S(1)} custom-call(s32[64]{0:T(128)S(1)} %get-tuple-element.6.order_ref, s32[64]{0:T(128)S(1)} %get-tuple-element.5.slot_ref, s32[1]{0:T(128)} %bitcast.count_ref, bf16[256,8,128]{2,1,0:T(8,128)(2,1)S(1)} %all-to-all-done.1.vis_ref), custom_call_target="tpu_custom_call" | custom-call | tf_op jit(solution)/shard_map/gridding/grid_blocks/pallas_call | solution.py:187
  58.4 0.0 copy-start.2
  58.4 0.0 copy-start.3
  58.4 0.0 copy-start.6
  58.4 0.0 copy-start.7
  58.5 21.2 %all_to_all.20.x_ref = bf16[16,2,32,512]{3,2,1,0:T(8,128)(2,1)S(1)} all-to-all(bf16[16,2,32,512]{3,2,1,0:T(8,128)(2,1)S(1)} %grid_blocks.1), channel_id=1, replica_groups=mesh['facet'=16,'span'=16] {'facet'}, dimensions={0} | all-to-all | bytes 2097152 | tf_op jit(solution)/shard_map/to_rows/all_to_all | solution.py:427
  79.7 0.0 copy-done.2
  79.7 0.0 copy-done.3
  79.7 0.0 copy-done.6
  79.7 0.0 copy-done.7
  79.7 2.0 %row_transform.1 = bf16[256,16,128]{2,1,0:T(8,128)(2,1)S(1)} custom-call(bf16[16,2,32,512]{3,2,1,0:T(8,128)(2,1)S(1)} %all_to_all.20.x_ref, bf16[256,256]{1,0:T(8,128)(2,1)S(1)} %copy-done.3, bf16[256,256]{1,0:T(8,128)(2,1)S(1)} %copy-done.2, f32[64,128]{1,0:T(8,128)S(1)} %copy-done.7, f32[64,128]{1,0:T(8,128)S(1)} %copy-done.6), custom_call_target="tpu_custom_call" | custom-call | tf_op jit(solution)/shard_map/rows_dft/row_transform/pallas_call | solution.py:294
  81.7 0.0 copy-start
  81.7 0.0 copy-start.1
  81.8 0.0 copy-start.4
  81.8 0.0 copy-start.5
  81.8 45.6 %all_to_all.21.x_ref = bf16[256,16,128]{2,1,0:T(8,128)(2,1)S(1)} all-to-all(bf16[256,16,128]{2,1,0:T(8,128)(2,1)S(1)} %row_transform.1), channel_id=1, replica_groups=mesh['facet'=16,'span'=16] {'facet','span'}, dimensions={0} | all-to-all | bytes 2097152 | tf_op jit(solution)/shard_map/to_columns/all_to_all | solution.py:431
  127.3 0.0 copy-done
  127.3 0.0 copy-done.1
  127.3 0.0 copy-done.4
  127.4 0.0 copy-done.5
  127.4 3.9 %column_transform.1 = f32[32,8192]{1,0:T(8,128)} custom-call(bf16[256,16,128]{2,1,0:T(8,128)(2,1)S(1)} %all_to_all.21.x_ref, f32[256,128]{1,0:T(8,128)S(1)} %copy-done.1, f32[256,128]{1,0:T(8,128)S(1)} %copy-done, bf16[128,256]{1,0:T(8,128)(2,1)S(1)} %copy-done.5, bf16[128,256]{1,0:T(8,128)(2,1)S(1)} %copy-done.4), custom_call_target="tpu_custom_call" | custom-call | tf_op jit(solution)/shard_map/columns_dft/column_transform/pallas_call | solution.py:355
  (2 shorter events, 0.0 us)
Async XLA Ops:
  2.4 7.7 %copy-start.8 = (s32[16,512]{1,0:T(8,128)S(1)}, s32[16,512]{1,0:T(8,128)}, u32[]{:S(2)}) copy-start(s32[16,512]{1,0:T(8,128)} %param.15) | copy-start | bytes 98308
  2.4 15.2 %all-to-all-start = ((bf16[16,32,256]{2,1,0:T(8,128)(2,1)}), bf16[16,32,256]{2,1,0:T(8,128)(2,1)S(1)}, u32[]{:S(2)}, u32[]{:S(2)}) async-start(bf16[16,32,256]{2,1,0:T(8,128)(2,1)} %rotate_blocks.1), calls=%async_computation | async-start | bytes 524288 | tf_op jit(solution)/shard_map/spread_span/all_to_all | solution.py:415
  19.2 34.2 %all-to-all-start.1 = ((bf16[256,8,128]{2,1,0:T(8,128)(2,1)}), bf16[256,8,128]{2,1,0:T(8,128)(2,1)S(1)}, u32[]{:S(2)}, u32[]{:S(2)}) async-start(bf16[256,8,128]{2,1,0:T(8,128)(2,1)} %pick_blocks.1), calls=%async_computation.1 | async-start | bytes 1048576 | tf_op jit(solution)/shard_map/to_owner/all_to_all | solution.py:421
  58.4 21.2 %copy-start.2 = (bf16[256,256]{1,0:T(8,128)(2,1)S(1)}, bf16[256,256]{1,0:T(8,128)(2,1)}, u32[]{:S(2)}) copy-start(bf16[256,256]{1,0:T(8,128)(2,1)} %constant.128.clone.dft_lo_ref) | copy-start | bytes 393220
  58.4 21.2 %copy-start.3 = (bf16[256,256]{1,0:T(8,128)(2,1)S(1)}, bf16[256,256]{1,0:T(8,128)(2,1)}, u32[]{:S(2)}) copy-start(bf16[256,256]{1,0:T(8,128)(2,1)} %constant.127.clone.dft_hi_ref) | copy-start | bytes 393220
  58.4 21.2 %copy-start.6 = (f32[64,128]{1,0:T(8,128)S(1)}, f32[64,128]{1,0:T(8,128)}, u32[]{:S(2)}) copy-start(f32[64,128]{1,0:T(8,128)} %constant.130.clone.sin_ref) | copy-start | bytes 98308
  58.4 21.2 %copy-start.7 = (f32[64,128]{1,0:T(8,128)S(1)}, f32[64,128]{1,0:T(8,128)}, u32[]{:S(2)}) copy-start(f32[64,128]{1,0:T(8,128)} %constant.129.clone.cos_ref) | copy-start | bytes 98308
  81.7 45.6 %copy-start = (f32[256,128]{1,0:T(8,128)S(1)}, f32[256,128]{1,0:T(8,128)}, u32[]{:S(2)}) copy-start(f32[256,128]{1,0:T(8,128)} %constant.132.clone.sin_ref) | copy-start | bytes 393220
  81.7 45.6 %copy-start.1 = (f32[256,128]{1,0:T(8,128)S(1)}, f32[256,128]{1,0:T(8,128)}, u32[]{:S(2)}) copy-start(f32[256,128]{1,0:T(8,128)} %constant.131.clone.cos_ref) | copy-start | bytes 393220
  81.8 45.6 %copy-start.4 = (bf16[128,256]{1,0:T(8,128)(2,1)S(1)}, bf16[128,256]{1,0:T(8,128)(2,1)}, u32[]{:S(2)}) copy-start(bf16[128,256]{1,0:T(8,128)(2,1)} %constant.134.clone.last_lo_ref) | copy-start | bytes 196612
  81.8 45.6 %copy-start.5 = (bf16[128,256]{1,0:T(8,128)(2,1)S(1)}, bf16[128,256]{1,0:T(8,128)(2,1)}, u32[]{:S(2)}) copy-start(bf16[128,256]{1,0:T(8,128)(2,1)} %constant.133.clone.last_hi_ref) | copy-start | bytes 196612

commit v5 on v4

--- a/solution.py
+++ b/solution.py
@@ -143,36 +143,56 @@
     cells = lax.broadcasted_iota(jnp.int32, (P_SIZE, 128), 0).astype(F32)
     count = count_ref[0]
 
-    def one_block(at, live):
-        entry = order_ref[at]
-        slot = slot_ref[at]
-        keep = jnp.where(live, 1.0, 0.0).astype(F32)
-        first = wide_ref[pl.ds(2 * entry, 16, stride=WIDE), :]
-        second = wide_ref[pl.ds(2 * entry + 1, 16, stride=WIDE), :]
-        total = None
+    def blocks_from(start, number, limit):
+        places = []
+        scales = []
+        for t in range(number):
+            entry = order_ref[start + t]
+            places.append(
+                (
+                    wide_ref[pl.ds(2 * entry, 16, stride=WIDE), :],
+                    wide_ref[pl.ds(2 * entry + 1, 16, stride=WIDE), :],
+                )
+            )
+            live = True if limit is None else start + t < limit
+            scales.append(None if limit is None else jnp.where(live, 1.0, 0.0).astype(F32))
+        totals = [None] * number
         for pair in range(4):
-            left = []
-            right = []
-            for k in (2 * pair, 2 * pair + 1):
-                real = (first[2 * k : 2 * k + 1] * keep).astype(BF16)
-                imag = (second[2 * k : 2 * k + 1] * keep).astype(BF16)
-                gap_u = cells - first[2 * k + 1 : 2 * k + 2]
-                row = jnp.exp2(gap_u * gap_u * GAUSS).astype(BF16)
-                left.append(jnp.concatenate([row * real, row * imag], axis=0))
-                gap_v = cells - second[2 * k + 1 : 2 * k + 2]
-                right.append(jnp.exp2(gap_v * gap_v * GAUSS).astype(BF16))
-            made = nt_dot(
-                jnp.concatenate(left, axis=1), jnp.concatenate(right, axis=1)
-            )
-            total = made if total is None else total + made
-        acc_ref[slot] += total.astype(BF16).astype(F32)
+            for t in range(number):
+                first, second = places[t]
+                left = []
+                right = []
+                for k in (2 * pair, 2 * pair + 1):
+                    real = first[2 * k : 2 * k + 1]
+                    imag = second[2 * k : 2 * k + 1]
+                    if scales[t] is not None:
+                        real = real * scales[t]
+                        imag = imag * scales[t]
+                    gap_u = cells - first[2 * k + 1 : 2 * k + 2]
+                    row = jnp.exp2(gap_u * gap_u * GAUSS).astype(BF16)
+                    left.append(
+                        jnp.concatenate([row * real.astype(BF16), row * imag.astype(BF16)], axis=0)
+                    )
+                    gap_v = cells - second[2 * k + 1 : 2 * k + 2]
+                    right.append(jnp.exp2(gap_v * gap_v * GAUSS).astype(BF16))
+                made = nt_dot(
+                    jnp.concatenate(left, axis=1), jnp.concatenate(right, axis=1)
+                )
+                totals[t] = made if totals[t] is None else totals[t] + made
+        for t in range(number):
+            acc_ref[slot_ref[start + t]] += totals[t].astype(BF16).astype(F32)
 
     def step(i, carry):
-        for t in range(STEP):
-            one_block(STEP * i + t, STEP * i + t < count)
+        blocks_from(STEP * i, STEP, None)
         return carry
 
-    lax.fori_loop(0, (count + STEP - 1) // STEP, step, 0)
+    def last(i, carry):
+        blocks_from(2 * i, 2, count)
+        return carry
+
+    whole = count // STEP
+    lax.fori_loop(0, whole, step, 0)
+    lax.fori_loop(whole * (STEP // 2), (count + 1) // 2, last, 0)
     for slot in range(BAND * BAND):
         sub_row, sub_col = divmod(slot, BAND)
         for part in range(2):
@@ -415,8 +435,9 @@
         spread = lax.all_to_all(parts, "facet", split_axis=0, concat_axis=0, tiled=True)
     with jax.named_scope("choose"):
         own_row = lax.dynamic_index_in_dim(sub_index, span_id, 0, keepdims=False)
+        order, slots, count = receive_table(sub_index, span_id, facet_id)
+        spread, order, slots, count = lax.optimization_barrier((spread, order, slots, count))
         chosen = pick_blocks(send_code(own_row), spread.reshape(-1, 256))
-        order, slots, count = receive_table(sub_index, span_id, facet_id)
     with jax.named_scope("to_owner"):
         arrived = lax.all_to_all(
             chosen, ("facet", "span"), split_axis=0, concat_axis=0, tiled=True

time: 131 us -> 129 us (0.985)
  blocking collectives: 66.8 us -> 98.9 us
  waiting for transfers between devices: 26.6 us -> 5.17 us
  starting transfers between devices: 20.5 us -> 7.72 us
    all_to_all x0 -> x1, blocking collectives: none -> 34 us  [shards(): lax.all_to_all(chosen, ('facet', 'span'), split_axis=0, concat_axis=0, ti...]
    all_to_all x1 -> x0, waiting for transfers between devices: 19.4 us -> none  [shards(): lax.all_to_all(chosen, ('facet', 'span'), split_axis=0, concat_axis=0, ti...]
    all_to_all x1 -> x0, starting transfers between devices: 12.8 us -> none  [shards(): lax.all_to_all(chosen, ('facet', 'span'), split_axis=0, concat_axis=0, ti...]
    all_to_all x1, waiting for transfers between devices: 7.17 us -> 5.17 us  [shards(): lax.all_to_all(parts, 'facet', split_axis=0, concat_axis=0, tiled=True)]
  transfers between devices with their start and end apart: 2 -> 1, of which waited for: 2 -> 1; matrix products, arithmetic and copies ran while one was open for 2% -> 2% of each run, Pallas kernels for 0% -> 0%
where the time goes in v5:
time: 129 us
  blocking collectives  98.9 us (77%)
  Pallas kernels  15.1 us (12%)
  starting transfers between devices  7.72 us (6%)
  waiting for transfers between devices  5.17 us (4%)
  other arithmetic  1.67 us (1%)
    all_to_all x1, blocking collectives, shards(): lax.all_to_all(half_done, ('facet', 'span'), split_axis=0, concat_axis=0,...  44.4 us
    all_to_all x1, blocking collectives, shards(): lax.all_to_all(chosen, ('facet', 'span'), split_axis=0, concat_axis=0, ti...  34 us
    all_to_all x1, blocking collectives, shards(): lax.all_to_all(block, 'facet', split_axis=0, concat_axis=0, tiled=True)  20.5 us
    all_to_all x1, starting transfers between devices, shards(): lax.all_to_all(parts, 'facet', split_axis=0, concat_axis=0, tiled=True)  7.72 us
    pallas_call x1, Pallas kernels, grid_blocks(): pl.pallas_call(grid_kernel, out_shape=jax.ShapeDtypeStruct((16, 2, 32, 51...  5.94 us
    all_to_all x1, waiting for transfers between devices, shards(): lax.all_to_all(parts, 'facet', split_axis=0, concat_axis=0, tiled=True)  5.17 us
    pallas_call x1, Pallas kernels, column_transform(): pl.pallas_call(column_kernel, out_shape=jax.ShapeDtypeStruct((32, N), F32...  3.88 us
  transfers between devices with their start and end apart: 1, of which 1 were waited for; matrix products, arithmetic and copies ran while one was open for 2% of the time, Pallas kernels for 0%

profile of v5, /device:TPU:1, one launch (start us, length us, event | category | flops | bytes accessed | tf_op | source)
XLA Modules:
  0.0 129.4 jit_solution(12310445571332671600)
XLA Ops:
  0.0 2.4 %rotate_blocks.1 = bf16[16,32,256]{2,1,0:T(8,128)(2,1)} custom-call(bf16[32,2,1024]{2,1,0:T(2,128)(2,1)} %bitcast.10, bf16[32,2,1024]{2,1,0:T(2,128)(2,1)} %bitcast.11, f32[32,1024]{1,0:T(8,128)} %bitcast.12), custom_call_target="tpu_custom_call" | custom-call | tf_op jit(solution)/shard_map/rotate/rotate_blocks/pallas_call | solution.py:104
  2.4 0.0 copy-start.8
  2.4 7.7 %all-to-all-start = ((bf16[16,32,256]{2,1,0:T(8,128)(2,1)}), bf16[16,32,256]{2,1,0:T(8,128)(2,1)S(1)}, u32[]{:S(2)}, u32[]{:S(2)}) async-start(bf16[16,32,256]{2,1,0:T(8,128)(2,1)} %rotate_blocks.1), calls=%async_computation | async-start | bytes 524288 | tf_op jit(solution)/shard_map/spread_span/all_to_all | solution.py:435
  10.2 0.0 copy-done.8
  10.2 0.1 fusion.7
  10.2 0.1 fusion.21
  10.3 0.1 fusion.13
  10.4 0.2 fusion.1
  10.6 0.2 fusion.3
  10.8 0.1 copy.13
  10.9 0.1 and.137
  11.0 0.1 convert_reduce_fusion.1
  11.1 0.2 select_reduce_fusion
  11.2 0.1 copy.14
  11.3 0.1 broadcast_in_dim.49
  11.4 0.2 convert_reduce_fusion
  11.6 0.1 select_reduce_fusion.1
  11.7 0.7 convert_reduce_fusion.2
  12.4 5.2 %all-to-all-done = bf16[16,32,256]{2,1,0:T(8,128)(2,1)S(1)} async-done(((bf16[16,32,256]{2,1,0:T(8,128)(2,1)}), bf16[16,32,256]{2,1,0:T(8,128)(2,1)S(1)}, u32[]{:S(2)}, u32[]{:S(2)}) %all-to-all-start) | async-done | bytes 262176 | tf_op jit(solution)/shard_map/spread_span/all_to_all | solution.py:435
  17.6 0.8 pick_blocks.1
  18.4 34.0 %all_to_all.20.vis_ref = bf16[256,8,128]{2,1,0:T(8,128)(2,1)S(1)} all-to-all(bf16[256,8,128]{2,1,0:T(8,128)(2,1)S(1)} %pick_blocks.1), channel_id=1, replica_groups=mesh['facet'=16,'span'=16] {'facet','span'}, dimensions={0} | all-to-all | bytes 1048576 | tf_op jit(solution)/shard_map/to_owner/all_to_all | solution.py:442
  52.4 5.9 %grid_blocks.1 = bf16[16,2,32,512]{3,2,1,0:T(8,128)(2,1)S(1)} custom-call(s32[64]{0:T(128)S(1)} %get-tuple-element.9.order_ref, s32[64]{0:T(128)S(1)} %get-tuple-element.10.slot_ref, s32[1]{0:T(128)} %bitcast.3.count_ref, bf16[256,8,128]{2,1,0:T(8,128)(2,1)S(1)} %all_to_all.20.vis_ref), custom_call_target="tpu_custom_call" | custom-call | tf_op jit(solution)/shard_map/gridding/grid_blocks/pallas_call | solution.py:207
  58.4 0.0 copy-start.2
  58.4 0.0 copy-start.3
  58.4 0.0 copy-start.6
  58.4 0.0 copy-start.7
  58.4 20.5 %all_to_all.21.x_ref = bf16[16,2,32,512]{3,2,1,0:T(8,128)(2,1)S(1)} all-to-all(bf16[16,2,32,512]{3,2,1,0:T(8,128)(2,1)S(1)} %grid_blocks.1), channel_id=1, replica_groups=mesh['facet'=16,'span'=16] {'facet'}, dimensions={0} | all-to-all | bytes 2097152 | tf_op jit(solution)/shard_map/to_rows/all_to_all | solution.py:448
  79.0 0.0 copy-done.2
  79.0 0.0 copy-done.3
  79.0 0.0 copy-done.6
  79.0 0.0 copy-done.7
  79.0 2.0 %row_transform.1 = bf16[256,16,128]{2,1,0:T(8,128)(2,1)S(1)} custom-call(bf16[16,2,32,512]{3,2,1,0:T(8,128)(2,1)S(1)} %all_to_all.21.x_ref, bf16[256,256]{1,0:T(8,128)(2,1)S(1)} %copy-done.3, bf16[256,256]{1,0:T(8,128)(2,1)S(1)} %copy-done.2, f32[64,128]{1,0:T(8,128)S(1)} %copy-done.7, f32[64,128]{1,0:T(8,128)S(1)} %copy-done.6), custom_call_target="tpu_custom_call" | custom-call | tf_op jit(solution)/shard_map/rows_dft/row_transform/pallas_call | solution.py:314
  81.0 0.0 copy-start
  81.0 0.0 copy-start.1
  81.0 0.0 copy-start.4
  81.1 0.0 copy-start.5
  81.1 44.4 %all_to_all.22.x_ref = bf16[256,16,128]{2,1,0:T(8,128)(2,1)S(1)} all-to-all(bf16[256,16,128]{2,1,0:T(8,128)(2,1)S(1)} %row_transform.1), channel_id=1, replica_groups=mesh['facet'=16,'span'=16] {'facet','span'}, dimensions={0} | all-to-all | bytes 2097152 | tf_op jit(solution)/shard_map/to_columns/all_to_all | solution.py:452
  125.5 0.0 copy-done
  125.5 0.0 copy-done.1
  125.5 0.0 copy-done.4
  125.5 0.0 copy-done.5
  125.5 3.9 %column_transform.1 = f32[32,8192]{1,0:T(8,128)} custom-call(bf16[256,16,128]{2,1,0:T(8,128)(2,1)S(1)} %all_to_all.22.x_ref, f32[256,128]{1,0:T(8,128)S(1)} %copy-done.1, f32[256,128]{1,0:T(8,128)S(1)} %copy-done, bf16[128,256]{1,0:T(8,128)(2,1)S(1)} %copy-done.5, bf16[128,256]{1,0:T(8,128)(2,1)S(1)} %copy-done.4), custom_call_target="tpu_custom_call" | custom-call | tf_op jit(solution)/shard_map/columns_dft/column_transform/pallas_call | solution.py:375
  (2 shorter events, 0.0 us)
Async XLA Ops:
  2.4 7.7 %copy-start.8 = (s32[16,512]{1,0:T(8,128)S(1)}, s32[16,512]{1,0:T(8,128)}, u32[]{:S(2)}) copy-start(s32[16,512]{1,0:T(8,128)} %param.15) | copy-start | bytes 98308
  2.4 15.2 %all-to-all-start = ((bf16[16,32,256]{2,1,0:T(8,128)(2,1)}), bf16[16,32,256]{2,1,0:T(8,128)(2,1)S(1)}, u32[]{:S(2)}, u32[]{:S(2)}) async-start(bf16[16,32,256]{2,1,0:T(8,128)(2,1)} %rotate_blocks.1), calls=%async_computation | async-start | bytes 524288 | tf_op jit(solution)/shard_map/spread_span/all_to_all | solution.py:435
  58.4 20.6 %copy-start.2 = (bf16[256,256]{1,0:T(8,128)(2,1)S(1)}, bf16[256,256]{1,0:T(8,128)(2,1)}, u32[]{:S(2)}) copy-start(bf16[256,256]{1,0:T(8,128)(2,1)} %constant.128.clone.dft_lo_ref) | copy-start | bytes 393220
  58.4 20.6 %copy-start.3 = (bf16[256,256]{1,0:T(8,128)(2,1)S(1)}, bf16[256,256]{1,0:T(8,128)(2,1)}, u32[]{:S(2)}) copy-start(bf16[256,256]{1,0:T(8,128)(2,1)} %constant.127.clone.dft_hi_ref) | copy-start | bytes 393220
  58.4 20.5 %copy-start.6 = (f32[64,128]{1,0:T(8,128)S(1)}, f32[64,128]{1,0:T(8,128)}, u32[]{:S(2)}) copy-start(f32[64,128]{1,0:T(8,128)} %constant.130.clone.sin_ref) | copy-start | bytes 98308
  58.4 20.5 %copy-start.7 = (f32[64,128]{1,0:T(8,128)S(1)}, f32[64,128]{1,0:T(8,128)}, u32[]{:S(2)}) copy-start(f32[64,128]{1,0:T(8,128)} %constant.129.clone.cos_ref) | copy-start | bytes 98308
  81.0 44.4 %copy-start = (f32[256,128]{1,0:T(8,128)S(1)}, f32[256,128]{1,0:T(8,128)}, u32[]{:S(2)}) copy-start(f32[256,128]{1,0:T(8,128)} %constant.132.clone.sin_ref) | copy-start | bytes 393220
  81.0 44.4 %copy-start.1 = (f32[256,128]{1,0:T(8,128)S(1)}, f32[256,128]{1,0:T(8,128)}, u32[]{:S(2)}) copy-start(f32[256,128]{1,0:T(8,128)} %constant.131.clone.cos_ref) | copy-start | bytes 393220
  81.0 44.4 %copy-start.4 = (bf16[128,256]{1,0:T(8,128)(2,1)S(1)}, bf16[128,256]{1,0:T(8,128)(2,1)}, u32[]{:S(2)}) copy-start(bf16[128,256]{1,0:T(8,128)(2,1)} %constant.134.clone.last_lo_ref) | copy-start | bytes 196612
  81.1 44.4 %copy-start.5 = (bf16[128,256]{1,0:T(8,128)(2,1)S(1)}, bf16[128,256]{1,0:T(8,128)(2,1)}, u32[]{:S(2)}) copy-start(bf16[128,256]{1,0:T(8,128)(2,1)} %constant.133.clone.last_hi_ref) | copy-start | bytes 196612

commit v6 on v5

--- a/solution.py
+++ b/solution.py
@@ -53,12 +53,11 @@
     last = np.concatenate(
         [np.kron(np.eye(4), cos_r), -np.kron(np.eye(4), sin_r)], axis=1
     )
-    last_hi, last_lo = split_table(last)
+    last_hi, _ = split_table(last)
     return (
         (twist_cos / N).astype(np.float32),
         (twist_sin / N).astype(np.float32),
         last_hi,
-        last_lo,
     )
 
 
@@ -328,7 +327,7 @@
 
 
 def column_kernel(
-    x_ref, cos_ref, sin_ref, last_hi_ref, last_lo_ref, out_ref, mid_ref, real_ref, imag_ref, put_ref
+    x_ref, cos_ref, sin_ref, last_hi_ref, out_ref, mid_ref, real_ref, imag_ref, put_ref
 ):
     for chunk in range(16):
         items = []
@@ -349,13 +348,12 @@
             real_ref[rows, :] = item[0] * cosine - item[1] * sine
             imag_ref[rows, :] = item[0] * sine + item[1] * cosine
     last_hi = last_hi_ref[...]
-    last_lo = last_lo_ref[...]
     for g in range(8):
         both = jnp.concatenate(
             [real_ref[g * GAP : g * GAP + 256, :], imag_ref[g * GAP : g * GAP + 256, :]], axis=1
         )
         high, low = split_value(both)
-        made = nt_dot(last_hi, high) + nt_dot(last_lo, high) + nt_dot(last_hi, low)
+        made = nt_dot(last_hi, high) + nt_dot(last_hi, low)
         for side in range(2):
             for m in range(4):
                 start = (side * 32 + 4 * g + m) * PAD

time: 129 us -> 129 us (level)
  no operation moved by 1% of the time
where the time goes in v6:
time: 129 us
  blocking collectives  98.2 us (76%)
  Pallas kernels  15.3 us (12%)
  starting transfers between devices  7.72 us (6%)
  waiting for transfers between devices  5.17 us (4%)
  other arithmetic  1.67 us (1%)
    all_to_all x1, blocking collectives, shards(): lax.all_to_all(half_done, ('facet', 'span'), split_axis=0, concat_axis=0,...  44 us
    all_to_all x1, blocking collectives, shards(): lax.all_to_all(chosen, ('facet', 'span'), split_axis=0, concat_axis=0, ti...  34 us
    all_to_all x1, blocking collectives, shards(): lax.all_to_all(block, 'facet', split_axis=0, concat_axis=0, tiled=True)  20.2 us
    all_to_all x1, starting transfers between devices, shards(): lax.all_to_all(parts, 'facet', split_axis=0, concat_axis=0, tiled=True)  7.72 us
    pallas_call x1, Pallas kernels, grid_blocks(): pl.pallas_call(grid_kernel, out_shape=jax.ShapeDtypeStruct((16, 2, 32, 51...  6.47 us
    all_to_all x1, waiting for transfers between devices, shards(): lax.all_to_all(parts, 'facet', split_axis=0, concat_axis=0, tiled=True)  5.17 us
    pallas_call x1, Pallas kernels, column_transform(): pl.pallas_call(column_kernel, out_shape=jax.ShapeDtypeStruct((32, N), F32...  3.5 us
  transfers between devices with their start and end apart: 1, of which 1 were waited for; matrix products, arithmetic and copies ran while one was open for 2% of the time, Pallas kernels for 0%

profile of v6, /device:TPU:1, one launch (start us, length us, event | category | flops | bytes accessed | tf_op | source)
XLA Modules:
  0.0 128.8 jit_solution(11592244628996519600)
XLA Ops:
  0.0 2.4 %rotate_blocks.1 = bf16[16,32,256]{2,1,0:T(8,128)(2,1)} custom-call(bf16[32,2,1024]{2,1,0:T(2,128)(2,1)} %bitcast.10, bf16[32,2,1024]{2,1,0:T(2,128)(2,1)} %bitcast.11, f32[32,1024]{1,0:T(8,128)} %bitcast.12), custom_call_target="tpu_custom_call" | custom-call | tf_op jit(solution)/shard_map/rotate/rotate_blocks/pallas_call | solution.py:103
  2.4 0.0 copy-start.7
  2.4 7.7 %all-to-all-start = ((bf16[16,32,256]{2,1,0:T(8,128)(2,1)}), bf16[16,32,256]{2,1,0:T(8,128)(2,1)S(1)}, u32[]{:S(2)}, u32[]{:S(2)}) async-start(bf16[16,32,256]{2,1,0:T(8,128)(2,1)} %rotate_blocks.1), calls=%async_computation | async-start | bytes 524288 | tf_op jit(solution)/shard_map/spread_span/all_to_all | solution.py:433
  10.2 0.0 copy-done.7
  10.2 0.1 fusion.7
  10.2 0.1 fusion.21
  10.3 0.1 fusion.13
  10.4 0.2 fusion.1
  10.6 0.2 fusion.3
  10.8 0.1 copy.12
  10.9 0.1 and.137
  11.0 0.1 convert_reduce_fusion.1
  11.1 0.2 select_reduce_fusion
  11.2 0.1 copy.13
  11.3 0.1 broadcast_in_dim.49
  11.4 0.2 convert_reduce_fusion
  11.6 0.1 select_reduce_fusion.1
  11.7 0.7 convert_reduce_fusion.2
  12.4 5.2 %all-to-all-done = bf16[16,32,256]{2,1,0:T(8,128)(2,1)S(1)} async-done(((bf16[16,32,256]{2,1,0:T(8,128)(2,1)}), bf16[16,32,256]{2,1,0:T(8,128)(2,1)S(1)}, u32[]{:S(2)}, u32[]{:S(2)}) %all-to-all-start) | async-done | bytes 262176 | tf_op jit(solution)/shard_map/spread_span/all_to_all | solution.py:433
  17.6 0.8 pick_blocks.1
  18.4 34.0 %all_to_all.20.vis_ref = bf16[256,8,128]{2,1,0:T(8,128)(2,1)S(1)} all-to-all(bf16[256,8,128]{2,1,0:T(8,128)(2,1)S(1)} %pick_blocks.1), channel_id=1, replica_groups=mesh['facet'=16,'span'=16] {'facet','span'}, dimensions={0} | all-to-all | bytes 1048576 | tf_op jit(solution)/shard_map/to_owner/all_to_all | solution.py:440
  52.4 6.5 %grid_blocks.1 = bf16[16,2,32,512]{3,2,1,0:T(8,128)(2,1)S(1)} custom-call(s32[64]{0:T(128)S(1)} %get-tuple-element.9.order_ref, s32[64]{0:T(128)S(1)} %get-tuple-element.10.slot_ref, s32[1]{0:T(128)} %bitcast.3.count_ref, bf16[256,8,128]{2,1,0:T(8,128)(2,1)S(1)} %all_to_all.20.vis_ref), custom_call_target="tpu_custom_call" | custom-call | tf_op jit(solution)/shard_map/gridding/grid_blocks/pallas_call | solution.py:206
  58.9 0.0 copy-start.2
  58.9 0.0 copy-start.3
  58.9 0.0 copy-start.5
  59.0 0.0 copy-start.6
  59.0 20.2 %all_to_all.21.x_ref = bf16[16,2,32,512]{3,2,1,0:T(8,128)(2,1)S(1)} all-to-all(bf16[16,2,32,512]{3,2,1,0:T(8,128)(2,1)S(1)} %grid_blocks.1), channel_id=1, replica_groups=mesh['facet'=16,'span'=16] {'facet'}, dimensions={0} | all-to-all | bytes 2097152 | tf_op jit(solution)/shard_map/to_rows/all_to_all | solution.py:446
  79.2 0.0 copy-done.2
  79.2 0.0 copy-done.3
  79.2 0.0 copy-done.5
  79.2 0.0 copy-done.6
  79.2 2.0 %row_transform.1 = bf16[256,16,128]{2,1,0:T(8,128)(2,1)S(1)} custom-call(bf16[16,2,32,512]{3,2,1,0:T(8,128)(2,1)S(1)} %all_to_all.21.x_ref, bf16[256,256]{1,0:T(8,128)(2,1)S(1)} %copy-done.3, bf16[256,256]{1,0:T(8,128)(2,1)S(1)} %copy-done.2, f32[64,128]{1,0:T(8,128)S(1)} %copy-done.6, f32[64,128]{1,0:T(8,128)S(1)} %copy-done.5), custom_call_target="tpu_custom_call" | custom-call | tf_op jit(solution)/shard_map/rows_dft/row_transform/pallas_call | solution.py:313
  81.3 0.0 copy-start
  81.3 0.0 copy-start.1
  81.3 0.0 copy-start.4
  81.3 44.0 %all_to_all.22.x_ref = bf16[256,16,128]{2,1,0:T(8,128)(2,1)S(1)} all-to-all(bf16[256,16,128]{2,1,0:T(8,128)(2,1)S(1)} %row_transform.1), channel_id=1, replica_groups=mesh['facet'=16,'span'=16] {'facet','span'}, dimensions={0} | all-to-all | bytes 2097152 | tf_op jit(solution)/shard_map/to_columns/all_to_all | solution.py:450
  125.3 0.0 copy-done
  125.3 0.0 copy-done.1
  125.3 0.0 copy-done.4
  125.3 3.5 %column_transform.1 = f32[32,8192]{1,0:T(8,128)} custom-call(bf16[256,16,128]{2,1,0:T(8,128)(2,1)S(1)} %all_to_all.22.x_ref, f32[256,128]{1,0:T(8,128)S(1)} %copy-done.1, f32[256,128]{1,0:T(8,128)S(1)} %copy-done, bf16[128,256]{1,0:T(8,128)(2,1)S(1)} %copy-done.4), custom_call_target="tpu_custom_call" | custom-call | tf_op jit(solution)/shard_map/columns_dft/column_transform/pallas_call | solution.py:373
  (2 shorter events, 0.0 us)
Async XLA Ops:
  2.4 7.7 %copy-start.7 = (s32[16,512]{1,0:T(8,128)S(1)}, s32[16,512]{1,0:T(8,128)}, u32[]{:S(2)}) copy-start(s32[16,512]{1,0:T(8,128)} %param.14) | copy-start | bytes 98308
  2.4 15.2 %all-to-all-start = ((bf16[16,32,256]{2,1,0:T(8,128)(2,1)}), bf16[16,32,256]{2,1,0:T(8,128)(2,1)S(1)}, u32[]{:S(2)}, u32[]{:S(2)}) async-start(bf16[16,32,256]{2,1,0:T(8,128)(2,1)} %rotate_blocks.1), calls=%async_computation | async-start | bytes 524288 | tf_op jit(solution)/shard_map/spread_span/all_to_all | solution.py:433
  58.9 20.3 %copy-start.2 = (bf16[256,256]{1,0:T(8,128)(2,1)S(1)}, bf16[256,256]{1,0:T(8,128)(2,1)}, u32[]{:S(2)}) copy-start(bf16[256,256]{1,0:T(8,128)(2,1)} %constant.126.clone.dft_lo_ref) | copy-start | bytes 393220
  58.9 20.3 %copy-start.3 = (bf16[256,256]{1,0:T(8,128)(2,1)S(1)}, bf16[256,256]{1,0:T(8,128)(2,1)}, u32[]{:S(2)}) copy-start(bf16[256,256]{1,0:T(8,128)(2,1)} %constant.125.clone.dft_hi_ref) | copy-start | bytes 393220
  58.9 20.2 %copy-start.5 = (f32[64,128]{1,0:T(8,128)S(1)}, f32[64,128]{1,0:T(8,128)}, u32[]{:S(2)}) copy-start(f32[64,128]{1,0:T(8,128)} %constant.128.clone.sin_ref) | copy-start | bytes 98308
  59.0 20.2 %copy-start.6 = (f32[64,128]{1,0:T(8,128)S(1)}, f32[64,128]{1,0:T(8,128)}, u32[]{:S(2)}) copy-start(f32[64,128]{1,0:T(8,128)} %constant.127.clone.cos_ref) | copy-start | bytes 98308
  81.3 44.0 %copy-start = (f32[256,128]{1,0:T(8,128)S(1)}, f32[256,128]{1,0:T(8,128)}, u32[]{:S(2)}) copy-start(f32[256,128]{1,0:T(8,128)} %constant.130.clone.sin_ref) | copy-start | bytes 393220
  81.3 44.0 %copy-start.1 = (f32[256,128]{1,0:T(8,128)S(1)}, f32[256,128]{1,0:T(8,128)}, u32[]{:S(2)}) copy-start(f32[256,128]{1,0:T(8,128)} %constant.129.clone.cos_ref) | copy-start | bytes 393220
  81.3 44.0 %copy-start.4 = (bf16[128,256]{1,0:T(8,128)(2,1)S(1)}, bf16[128,256]{1,0:T(8,128)(2,1)}, u32[]{:S(2)}) copy-start(bf16[128,256]{1,0:T(8,128)(2,1)} %constant.131.clone.last_hi_ref) | copy-start | bytes 196612

commit v7 on v6

--- a/solution.py
+++ b/solution.py
@@ -39,11 +39,11 @@
 
 
 def row_tables():
-    dft_hi, dft_lo = split_table(
+    dft_hi, _ = split_table(
         complex_matrix(*angle_tables(np.arange(128), np.arange(128), 128))
     )
     twist_cos, twist_sin = angle_tables(np.arange(64), np.arange(128), N)
-    return dft_hi, dft_lo, twist_cos.astype(np.float32), twist_sin.astype(np.float32)
+    return dft_hi, twist_cos.astype(np.float32), twist_sin.astype(np.float32)
 
 
 def column_tables():
@@ -266,7 +266,7 @@
 
 
 def row_kernel(
-    x_ref, dft_hi_ref, dft_lo_ref, cos_ref, sin_ref, out_ref, mid_ref, hi_ref, lo_ref, put_ref
+    x_ref, dft_hi_ref, cos_ref, sin_ref, out_ref, mid_ref, hi_ref, lo_ref, put_ref
 ):
     for half in range(2):
         rows = pl.ds(16 * half, 16)
@@ -293,11 +293,10 @@
             hi_ref[a * 32 : (a + 1) * 32, :] = high
             lo_ref[a * 32 : (a + 1) * 32, :] = low
     dft_hi = dft_hi_ref[...]
-    dft_lo = dft_lo_ref[...]
     for n in range(8):
         high = hi_ref[n * 256 : (n + 1) * 256, :]
         low = lo_ref[n * 256 : (n + 1) * 256, :]
-        made = nt_dot(dft_hi, high) + nt_dot(dft_lo, high) + nt_dot(dft_hi, low)
+        made = nt_dot(dft_hi, high) + nt_dot(dft_hi, low)
         for part in range(2):
             for piece in range(2):
                 half, i = divmod(2 * n + piece, 8)

time: 129 us -> 129 us (level)
  Pallas kernels: 15.3 us -> 13.4 us
  blocking collectives: 98.2 us -> 100 us
    all_to_all x1, blocking collectives: 44 us -> 47.7 us  [shards(): lax.all_to_all(half_done, ('facet', 'span'), split_axis=0, concat_axis=0,...]
    pallas_call x1, Pallas kernels: 6.47 us -> 4.83 us  [grid_blocks(): pl.pallas_call(grid_kernel, out_shape=jax.ShapeDtypeStruct((16, 2, 32, 51...]
    all_to_all x1, blocking collectives: 20.2 us -> 18.6 us  [shards(): lax.all_to_all(block, 'facet', split_axis=0, concat_axis=0, tiled=True)]
where the time goes in v7:
time: 129 us
  blocking collectives  100 us (78%)
  Pallas kernels  13.4 us (10%)
  starting transfers between devices  7.72 us (6%)
  waiting for transfers between devices  5.17 us (4%)
  other arithmetic  1.67 us (1%)
    all_to_all x1, blocking collectives, shards(): lax.all_to_all(half_done, ('facet', 'span'), split_axis=0, concat_axis=0,...  47.7 us
    all_to_all x1, blocking collectives, shards(): lax.all_to_all(chosen, ('facet', 'span'), split_axis=0, concat_axis=0, ti...  34 us
    all_to_all x1, blocking collectives, shards(): lax.all_to_all(block, 'facet', split_axis=0, concat_axis=0, tiled=True)  18.6 us
    all_to_all x1, starting transfers between devices, shards(): lax.all_to_all(parts, 'facet', split_axis=0, concat_axis=0, tiled=True)  7.72 us
    all_to_all x1, waiting for transfers between devices, shards(): lax.all_to_all(parts, 'facet', split_axis=0, concat_axis=0, tiled=True)  5.17 us
    pallas_call x1, Pallas kernels, grid_blocks(): pl.pallas_call(grid_kernel, out_shape=jax.ShapeDtypeStruct((16, 2, 32, 51...  4.83 us
    pallas_call x1, Pallas kernels, column_transform(): pl.pallas_call(column_kernel, out_shape=jax.ShapeDtypeStruct((32, N), F32...  3.5 us
  transfers between devices with their start and end apart: 1, of which 1 were waited for; matrix products, arithmetic and copies ran while one was open for 2% of the time, Pallas kernels for 0%

profile of v7, /device:TPU:1, one launch (start us, length us, event | category | flops | bytes accessed | tf_op | source)
XLA Modules:
  0.0 129.0 jit_solution(8507887917064857582)
XLA Ops:
  0.0 2.4 %rotate_blocks.1 = bf16[16,32,256]{2,1,0:T(8,128)(2,1)} custom-call(bf16[32,2,1024]{2,1,0:T(2,128)(2,1)} %bitcast.10, bf16[32,2,1024]{2,1,0:T(2,128)(2,1)} %bitcast.11, f32[32,1024]{1,0:T(8,128)} %bitcast.12), custom_call_target="tpu_custom_call" | custom-call | tf_op jit(solution)/shard_map/rotate/rotate_blocks/pallas_call | solution.py:103
  2.4 0.0 copy-start.6
  2.4 7.7 %all-to-all-start = ((bf16[16,32,256]{2,1,0:T(8,128)(2,1)}), bf16[16,32,256]{2,1,0:T(8,128)(2,1)S(1)}, u32[]{:S(2)}, u32[]{:S(2)}) async-start(bf16[16,32,256]{2,1,0:T(8,128)(2,1)} %rotate_blocks.1), calls=%async_computation | async-start | bytes 524288 | tf_op jit(solution)/shard_map/spread_span/all_to_all | solution.py:432
  10.2 0.0 copy-done.6
  10.2 0.1 fusion.7
  10.2 0.1 fusion.21
  10.3 0.1 fusion.13
  10.4 0.2 fusion.1
  10.6 0.2 fusion.3
  10.8 0.1 copy.11
  10.9 0.1 and.137
  11.0 0.1 convert_reduce_fusion.1
  11.1 0.2 select_reduce_fusion
  11.2 0.1 copy.12
  11.3 0.1 broadcast_in_dim.49
  11.4 0.2 convert_reduce_fusion
  11.6 0.1 select_reduce_fusion.1
  11.7 0.7 convert_reduce_fusion.2
  12.4 5.2 %all-to-all-done = bf16[16,32,256]{2,1,0:T(8,128)(2,1)S(1)} async-done(((bf16[16,32,256]{2,1,0:T(8,128)(2,1)}), bf16[16,32,256]{2,1,0:T(8,128)(2,1)S(1)}, u32[]{:S(2)}, u32[]{:S(2)}) %all-to-all-start) | async-done | bytes 262176 | tf_op jit(solution)/shard_map/spread_span/all_to_all | solution.py:432
  17.6 0.8 pick_blocks.1
  18.4 34.0 %all_to_all.20.vis_ref = bf16[256,8,128]{2,1,0:T(8,128)(2,1)S(1)} all-to-all(bf16[256,8,128]{2,1,0:T(8,128)(2,1)S(1)} %pick_blocks.1), channel_id=1, replica_groups=mesh['facet'=16,'span'=16] {'facet','span'}, dimensions={0} | all-to-all | bytes 1048576 | tf_op jit(solution)/shard_map/to_owner/all_to_all | solution.py:439
  52.4 4.8 %grid_blocks.1 = bf16[16,2,32,512]{3,2,1,0:T(8,128)(2,1)S(1)} custom-call(s32[64]{0:T(128)S(1)} %get-tuple-element.9.order_ref, s32[64]{0:T(128)S(1)} %get-tuple-element.10.slot_ref, s32[1]{0:T(128)} %bitcast.3.count_ref, bf16[256,8,128]{2,1,0:T(8,128)(2,1)S(1)} %all_to_all.20.vis_ref), custom_call_target="tpu_custom_call" | custom-call | tf_op jit(solution)/shard_map/gridding/grid_blocks/pallas_call | solution.py:206
  57.3 0.0 copy-start.2
  57.3 0.0 copy-start.4
  57.3 0.0 copy-start.5
  57.3 18.6 %all_to_all.21.x_ref = bf16[16,2,32,512]{3,2,1,0:T(8,128)(2,1)S(1)} all-to-all(bf16[16,2,32,512]{3,2,1,0:T(8,128)(2,1)S(1)} %grid_blocks.1), channel_id=1, replica_groups=mesh['facet'=16,'span'=16] {'facet'}, dimensions={0} | all-to-all | bytes 2097152 | tf_op jit(solution)/shard_map/to_rows/all_to_all | solution.py:445
  75.9 0.0 copy-done.2
  75.9 0.0 copy-done.4
  75.9 0.0 copy-done.5
  75.9 1.8 %row_transform.1 = bf16[256,16,128]{2,1,0:T(8,128)(2,1)S(1)} custom-call(bf16[16,2,32,512]{3,2,1,0:T(8,128)(2,1)S(1)} %all_to_all.21.x_ref, bf16[256,256]{1,0:T(8,128)(2,1)S(1)} %copy-done.2, f32[64,128]{1,0:T(8,128)S(1)} %copy-done.5, f32[64,128]{1,0:T(8,128)S(1)} %copy-done.4), custom_call_target="tpu_custom_call" | custom-call | tf_op jit(solution)/shard_map/rows_dft/row_transform/pallas_call | solution.py:312
  77.8 0.0 copy-start
  77.8 0.0 copy-start.1
  77.8 0.0 copy-start.3
  77.8 47.7 %all_to_all.22.x_ref = bf16[256,16,128]{2,1,0:T(8,128)(2,1)S(1)} all-to-all(bf16[256,16,128]{2,1,0:T(8,128)(2,1)S(1)} %row_transform.1), channel_id=1, replica_groups=mesh['facet'=16,'span'=16] {'facet','span'}, dimensions={0} | all-to-all | bytes 2097152 | tf_op jit(solution)/shard_map/to_columns/all_to_all | solution.py:449
  125.5 0.0 copy-done
  125.5 0.0 copy-done.1
  125.5 0.0 copy-done.3
  125.5 3.5 %column_transform.1 = f32[32,8192]{1,0:T(8,128)} custom-call(bf16[256,16,128]{2,1,0:T(8,128)(2,1)S(1)} %all_to_all.22.x_ref, f32[256,128]{1,0:T(8,128)S(1)} %copy-done.1, f32[256,128]{1,0:T(8,128)S(1)} %copy-done, bf16[128,256]{1,0:T(8,128)(2,1)S(1)} %copy-done.3), custom_call_target="tpu_custom_call" | custom-call | tf_op jit(solution)/shard_map/columns_dft/column_transform/pallas_call | solution.py:372
  (2 shorter events, 0.0 us)
Async XLA Ops:
  2.4 7.7 %copy-start.6 = (s32[16,512]{1,0:T(8,128)S(1)}, s32[16,512]{1,0:T(8,128)}, u32[]{:S(2)}) copy-start(s32[16,512]{1,0:T(8,128)} %param.13) | copy-start | bytes 98308
  2.4 15.2 %all-to-all-start = ((bf16[16,32,256]{2,1,0:T(8,128)(2,1)}), bf16[16,32,256]{2,1,0:T(8,128)(2,1)S(1)}, u32[]{:S(2)}, u32[]{:S(2)}) async-start(bf16[16,32,256]{2,1,0:T(8,128)(2,1)} %rotate_blocks.1), calls=%async_computation | async-start | bytes 524288 | tf_op jit(solution)/shard_map/spread_span/all_to_all | solution.py:432
  57.3 18.7 %copy-start.2 = (bf16[256,256]{1,0:T(8,128)(2,1)S(1)}, bf16[256,256]{1,0:T(8,128)(2,1)}, u32[]{:S(2)}) copy-start(bf16[256,256]{1,0:T(8,128)(2,1)} %constant.123.clone.dft_hi_ref) | copy-start | bytes 393220
  57.3 18.6 %copy-start.4 = (f32[64,128]{1,0:T(8,128)S(1)}, f32[64,128]{1,0:T(8,128)}, u32[]{:S(2)}) copy-start(f32[64,128]{1,0:T(8,128)} %constant.125.clone.sin_ref) | copy-start | bytes 98308
  57.3 18.6 %copy-start.5 = (f32[64,128]{1,0:T(8,128)S(1)}, f32[64,128]{1,0:T(8,128)}, u32[]{:S(2)}) copy-start(f32[64,128]{1,0:T(8,128)} %constant.124.clone.cos_ref) | copy-start | bytes 98308
  77.8 47.7 %copy-start = (f32[256,128]{1,0:T(8,128)S(1)}, f32[256,128]{1,0:T(8,128)}, u32[]{:S(2)}) copy-start(f32[256,128]{1,0:T(8,128)} %constant.127.clone.sin_ref) | copy-start | bytes 393220
  77.8 47.7 %copy-start.1 = (f32[256,128]{1,0:T(8,128)S(1)}, f32[256,128]{1,0:T(8,128)}, u32[]{:S(2)}) copy-start(f32[256,128]{1,0:T(8,128)} %constant.126.clone.cos_ref) | copy-start | bytes 393220
  77.8 47.7 %copy-start.3 = (bf16[128,256]{1,0:T(8,128)(2,1)S(1)}, bf16[128,256]{1,0:T(8,128)(2,1)}, u32[]{:S(2)}) copy-start(bf16[128,256]{1,0:T(8,128)(2,1)} %constant.128.clone.last_hi_ref) | copy-start | bytes 196612
